TPU v7x, 256 devices: a whole 4x4x8 slice. The times are simulated.
256 devices in a mesh: row: 32 (over x, y, core), col: 8 (over z).
Axes of the slice: x: 4, y: 4, z: 8, core: 2. Of those that a mesh axis runs over, the one named last changes fastest.
Arguments:
- object_field: float32 [2, 24576, 4096], P(None, 'row', 'col'), may hold values from -6 to 6
- probe: float32 [2, 256, 256], replicated, may hold values from -6 to 6
- amplitudes: bfloat16 [32, 8, 3, 4, 256, 256], P('row', 'col'), may hold values from 0 to 2
- positions: int32 [32, 8, 3, 4, 2], P('row', 'col'), may hold values from -128 to 640, as said below
- counts: int32 [32, 8, 3], P('row', 'col'), may hold values from 1 to 4, as said below
Outputs:
- gradient: float32 [2, 24576, 4096], P(None, 'row', 'col')
- updated_object: float32 [2, 24576, 4096], P(None, 'row', 'col')
Inputs may be any that keep to these rules, and one draw needn't show every extreme that they name: `positions`: offsets lie from -128 to 640 for rows and from -128 to 384 for columns. In every tile slot 0 of micro-batch 0 sits at row -128 and column 384, and slot 0 of micro-batch 1 at row 640 and column -128. `counts`: slots 0 to count - 1 are live. Some tile has 4 live slots in every micro-batch.
All inputs are finite; a program needn't handle non-finite values.
Results may differ from a plain program's by a relative error of at most 0.0059.
Values may be sent and summed in bfloat16 or wider, within the bound.
No kernel may reach another device: no remote copies, remote signals or barrier semaphores. Data moves between devices by JAX's collectives and lax.ppermute only.
A program may use at most 128 MiB of HBM per device.

v0:
```python
import math

import jax
import jax.numpy as jnp
from jax import lax
from jax.experimental import pallas as pl
from jax.experimental.pallas import tpu as pltpu
from jax.sharding import PartitionSpec as P

step_scale = 0.5
LANES = 128
PACK = 16
CHUNK = 32
GROUP = 2
f32 = jnp.float32
bf16 = jnp.bfloat16
VMEM = pl.BlockSpec(memory_space=pltpu.VMEM)
SMEM = pl.BlockSpec(memory_space=pltpu.SMEM)
ANY = pl.BlockSpec(memory_space=pl.ANY)


def swap(block, axis, parity):
    size = lax.axis_size(axis)
    route = []
    for i in range(parity, size - 1, 2):
        route += [(i, i + 1), (i + 1, i)]
    return lax.ppermute(block, axis, route)


def even(axis):
    return lax.rem(lax.axis_index(axis), 2) == 0


def dft_parts(window):
    counter = jnp.arange(window, dtype=jnp.int32)
    product = counter[:, None] * counter[None, :] % window
    angles = 2.0 * math.pi / window * product.astype(f32)
    scale_value = 1.0 / math.sqrt(window)
    return (
        (jnp.cos(angles) * scale_value).astype(bf16),
        (-jnp.sin(angles) * scale_value).astype(bf16),
    )


def meta_rows(pos_ref, counts_ref):
    slots = pos_ref.shape[0] // 2
    lane = lax.broadcasted_iota(jnp.int32, (PACK, LANES), 1)
    row = jnp.zeros((PACK, LANES), jnp.int32)
    for k in range(2 * slots):
        value = pos_ref[k] + LANES
        row = jnp.where(lane == k, value // 16, row)
        row = jnp.where(lane == 2 * slots + k, lax.rem(value, 16), row)
    for k in range(counts_ref.shape[0]):
        row = jnp.where(lane == 4 * slots + k, counts_ref[k], row)
    return row.astype(f32).astype(bf16)


def edges_kernel(pos_ref, counts_ref, obj_hbm, first_ref, second_ref, low, high, sem):
    tile_r, tile_c = obj_hbm.shape[1:]
    copies = []
    for c in range(2):
        copies.append(pltpu.make_async_copy(obj_hbm.at[c, :, pl.ds(0, LANES)], low.at[c], sem.at[0, c]))
        copies.append(
            pltpu.make_async_copy(obj_hbm.at[c, :, pl.ds(tile_c - LANES, LANES)], high.at[c], sem.at[1, c])
        )
    for copy in copies:
        copy.start()
    upward = even("col")
    meta = meta_rows(pos_ref, counts_ref)
    first_ref[2 * tile_r :, :] = meta
    second_ref[2 * tile_r :, :] = meta
    for copy in copies:
        copy.wait()
    for c in range(2):
        for r in range(0, tile_r, 128):
            a = low[c, r : r + 128, :]
            b = high[c, r : r + 128, :]
            rows = slice(c * tile_r + r, c * tile_r + r + 128)
            first_ref[rows, :] = jnp.where(upward, b, a).astype(bf16)
            second_ref[rows, :] = jnp.where(upward, a, b).astype(bf16)


def prepare_kernel(obj_hbm, obj_ref, canvas_ref, sem):
    tile_r, tile_c = obj_hbm.shape[1:]
    margin = (obj_ref.shape[2] - tile_r) // 2
    tiles = tile_c // LANES
    body = pl.ds(margin, tile_r)
    copies = [
        pltpu.make_async_copy(
            obj_hbm.at[c, :, pl.ds(LANES * t, LANES)], obj_ref.at[c, t + 1, body, :], sem.at[c, t]
        )
        for c in range(2)
        for t in range(tiles)
    ]
    for copy in copies:
        copy.start()
    canvas_ref[...] = jnp.zeros_like(canvas_ref)
    for k, copy in enumerate(copies):
        copy.wait()
        c, t = divmod(k, tiles)
        obj_ref[c, t + 1, body, :] = obj_ref[c, t + 1, body, :].astype(bf16).astype(f32)


def sides_kernel(obj_in, za_ref, zb_ref, obj_ref, ya_ref, yb_ref):
    tiles = obj_ref.shape[1] - 2
    margin = LANES
    tile_r = obj_ref.shape[2] - 2 * margin
    right_first = even("col")
    downward = even("row")
    for c in range(2):
        for r in range(0, tile_r, 128):
            rows = slice(c * tile_r + r, c * tile_r + r + 128)
            a = za_ref[rows, :].astype(f32)
            b = zb_ref[rows, :].astype(f32)
            at = slice(margin + r, margin + r + 128)
            obj_ref[c, 0, at, :] = jnp.where(right_first, b, a)
            obj_ref[c, tiles + 1, at, :] = jnp.where(right_first, a, b)
    for c in range(2):
        for t in range(tiles + 2):
            top = obj_ref[c, t, margin : 2 * margin, :]
            bottom = obj_ref[c, t, tile_r : tile_r + margin, :]
            k = (c * (tiles + 2) + t) * margin
            ya_ref[k : k + margin, :] = jnp.where(downward, bottom, top).astype(bf16)
            yb_ref[k : k + margin, :] = jnp.where(downward, top, bottom).astype(bf16)


def slots_kernel(
    pos_ref, counts_ref, obj_in, canvas_in, ya_ref, yb_ref, probe_ref, amp_ref, fwd_ref, bwd_ref, ext_ref,
    obj, canvas_ref, ra_ref, rb_ref,
    todo, prb, xs, hs, er,
):
    batches = counts_ref.shape[0]
    slots = pos_ref.shape[0] // (2 * batches)
    win = probe_ref.shape[1]
    margin = win // 2
    tiles = obj.shape[1] - 2
    tile_r = obj.shape[2] - 2 * margin
    lower_first = even("row")
    for c in range(2):
        for t in range(tiles + 2):
            k = (c * (tiles + 2) + t) * margin
            a = ya_ref[k : k + margin, :].astype(f32)
            b = yb_ref[k : k + margin, :].astype(f32)
            obj[c, t, 0:margin, :] = jnp.where(lower_first, b, a)
            obj[c, t, margin + tile_r :, :] = jnp.where(lower_first, a, b)

    def collect(slot, count):
        batch = slot // slots
        live = slot - batch * slots < counts_ref[batch]

        @pl.when(live)
        def _():
            todo[count] = slot

        return count + live.astype(jnp.int32)

    total = lax.fori_loop(0, batches * slots, collect, jnp.int32(0))
    lane = lax.broadcasted_iota(jnp.int32, (CHUNK, LANES), 1)

    def group(p, carry):
        chosen = []
        for g in range(GROUP):
            at = p * GROUP + g
            slot = todo[jnp.minimum(at, total - 1)]
            row = pos_ref[2 * slot] + margin
            col = pos_ref[2 * slot + 1] + margin
            tile = col // LANES
            shift = col - tile * LANES
            chosen.append((slot, row, tile, jnp.minimum(tile + 2, tiles + 1), shift, at < total))

        def exit_waves(g):
            slot, row, tile, wrapped, shift, valid = chosen[g]
            low = lane < shift
            for i in range(0, win, CHUNK):
                turned = []
                window = []
                for c in range(2):
                    one = pltpu.roll(probe_ref[c, i : i + CHUNK, 0:LANES], shift, 1)
                    two = pltpu.roll(probe_ref[c, i : i + CHUNK, LANES:], shift, 1)
                    turned.append((jnp.where(low, two, one), jnp.where(low, one, two)))
                    at = pl.ds(row + i, CHUNK)
                    window.append(
                        (jnp.where(low, obj[c, wrapped, at, :], obj[c, tile, at, :]), obj[c, tile + 1, at, :])
                    )
                for h in range(2):
                    pr, pi = turned[0][h], turned[1][h]
                    wr, wi = window[0][h], window[1][h]
                    prb[g, 0, h, i : i + CHUNK, :] = pr
                    prb[g, 1, h, i : i + CHUNK, :] = pi
                    cols = slice(win * g + LANES * h, win * g + LANES * (h + 1))
                    xs[i : i + CHUNK, cols] = (pr * wr - pi * wi).astype(bf16)
                    xs[win + i : win + i + CHUNK, cols] = (pr * wi + pi * wr).astype(bf16)

        def rolled_table(g):
            shift = chosen[g][4]
            for i in range(0, win, CHUNK):
                for h in range(2):
                    real = ext_ref[0, h, pl.ds(win - shift + i, CHUNK), :].astype(bf16)
                    imag = ext_ref[1, h, pl.ds(win - shift + i, CHUNK), :].astype(bf16)
                    a = slice(LANES * h, LANES * (h + 1))
                    b = slice(win + LANES * h, win + LANES * (h + 1))
                    er[g, i : i + CHUNK, a] = real
                    er[g, i : i + CHUNK, b] = imag
                    er[g, win + i : win + i + CHUNK, a] = -imag
                    er[g, win + i : win + i + CHUNK, b] = real

        def rows_dft(table_ref):
            for g in range(GROUP):
                for part in range(2):
                    out = jnp.dot(
                        table_ref[win * part : win * (part + 1), :],
                        xs[:, win * g : win * (g + 1)],
                        preferred_element_type=f32,
                    )
                    hs[g, :, win * part : win * (part + 1)] = out.astype(bf16)

        def residual_waves(g):
            far = jnp.dot(hs[g], er[g], preferred_element_type=f32)
            real, imag = far[:, :win], far[:, win:]
            scale = 1.0 - amp_ref[chosen[g][0]].astype(f32) * lax.rsqrt(real * real + imag * imag + 1.0)
            xs[:win, win * g : win * (g + 1)] = (real * scale).astype(bf16)
            xs[win:, win * g : win * (g + 1)] = (imag * scale).astype(bf16)

        def accumulate(g):
            slot, row, tile, wrapped, shift, valid = chosen[g]
            back = lax.dot_general(hs[g], er[g], (((1,), (1,)), ((), ())), preferred_element_type=f32)
            keep = lax.broadcasted_iota(jnp.int32, (win, LANES), 1) < shift
            at = pl.ds(row, win)
            for h in range(2):
                pr, pi = prb[g, 0, h], prb[g, 1, h]
                br = back[:, LANES * h : LANES * (h + 1)]
                bi = back[:, win + LANES * h : win + LANES * (h + 1)]
                terms = [pr * br + pi * bi, pr * bi - pi * br]
                if g:
                    terms = [jnp.where(valid, term, 0.0) for term in terms]
                for c in range(2):
                    if h == 0:
                        canvas_ref[c, tile, at, :] += jnp.where(keep, 0.0, terms[c])
                        canvas_ref[c, wrapped, at, :] += jnp.where(keep, terms[c], 0.0)
                    else:
                        canvas_ref[c, tile + 1, at, :] += terms[c]

        for g in range(GROUP):
            exit_waves(g)
        rows_dft(fwd_ref)
        for g in range(GROUP):
            rolled_table(g)
        for g in range(GROUP):
            residual_waves(g)
        rows_dft(bwd_ref)
        for g in range(GROUP):
            accumulate(g)
        return carry

    lax.fori_loop(0, (total + GROUP - 1) // GROUP, group, 0)

    for c in range(2):
        for t in range(tiles + 2):
            k = (c * (tiles + 2) + t) * margin
            top = canvas_ref[c, t, 0:margin, :]
            bottom = canvas_ref[c, t, margin + tile_r :, :]
            ra_ref[k : k + margin, :] = jnp.where(lower_first, bottom, top).astype(bf16)
            rb_ref[k : k + margin, :] = jnp.where(lower_first, top, bottom).astype(bf16)


def light_kernel(meta_ref, probe_ref, scale_ref, power, light):
    win = probe_ref.shape[1]
    tiles, tile_r = scale_ref.shape[:2]
    tile_c = tiles * LANES
    fields = 51
    batches = 3
    slots = 4
    light[...] = jnp.zeros_like(light)
    for h in range(2):
        cols = slice(LANES * h, LANES * (h + 1))
        real, imag = probe_ref[0, :, cols], probe_ref[1, :, cols]
        power[h] = real * real + imag * imag
    step = 2 * batches * slots

    def tile_slots(n, carry):
        down = n // 3 - 1
        across = n - (down + 1) * 3 - 1

        def one(slot, inner):
            batch = slot // slots
            row = meta_ref[n, 2 * slot] * 16 + meta_ref[n, step + 2 * slot] - LANES + down * tile_r
            col = meta_ref[n, 2 * slot + 1] * 16 + meta_ref[n, step + 2 * slot + 1] - LANES + across * tile_c
            live = slot - batch * slots < meta_ref[n, 2 * step + batch]
            meets = (row > -win) & (row < tile_r) & (col > -win) & (col < tile_c)

            @pl.when(live & meets)
            def _():
                place = col + win
                tile = place // LANES
                shift = place - tile * LANES
                for i in range(0, win, 64):
                    low = lax.broadcasted_iota(jnp.int32, (64, LANES), 1) < shift
                    one_half = pltpu.roll(power[0, i : i + 64, :], shift, 1)
                    two_half = pltpu.roll(power[1, i : i + 64, :], shift, 1)
                    at = pl.ds(row + win + i, 64)
                    light[tile, at, :] += jnp.where(low, 0.0, one_half)
                    light[tile + 1, at, :] += jnp.where(low, one_half, two_half)
                    light[tile + 2, at, :] += jnp.where(low, two_half, 0.0)

            return inner

        return lax.fori_loop(0, batches * slots, one, carry)

    lax.fori_loop(0, 9, tile_slots, 0)
    for t in range(tiles):
        scale_ref[t] = step_scale / (light[t + 2, win : win + tile_r, :] + 1.0)


def strips_kernel(canvas_ref, ya_ref, yb_ref, sa_ref, sb_ref):
    tiles = canvas_ref.shape[1] - 2
    margin = LANES
    tile_r = canvas_ref.shape[2] - 2 * margin
    lower_first = even("row")
    right_first = even("col")
    for c in range(2):
        for r in range(0, tile_r, margin):
            sides = []
            for t in (0, tiles + 1):
                value = canvas_ref[c, t, margin + r : 2 * margin + r, :]
                k = (c * (tiles + 2) + t) * margin
                a, b = ya_ref[k : k + margin, :].astype(f32), yb_ref[k : k + margin, :].astype(f32)
                if r == 0:
                    value += jnp.where(lower_first, b, a)
                if r == tile_r - margin:
                    value += jnp.where(lower_first, a, b)
                sides.append(value)
            rows = slice(c * tile_r + r, c * tile_r + r + margin)
            sa_ref[rows, :] = jnp.where(right_first, sides[1], sides[0]).astype(bf16)
            sb_ref[rows, :] = jnp.where(right_first, sides[0], sides[1]).astype(bf16)


def update_kernel(obj_ref, canvas_ref, ya_ref, yb_ref, sa_ref, sb_ref, scale_ref, grad_ref, out_ref):
    tiles = canvas_ref.shape[1] - 2
    margin = LANES
    tile_r = canvas_ref.shape[2] - 2 * margin
    step = pl.program_id(0)
    lower_first = even("row")
    right_first = even("col")
    first = step == 0
    last = step == pl.num_programs(0) - 1
    start = pl.multiple_of(step * margin, margin)
    for c in range(2):
        for t in range(tiles):
            value = canvas_ref[c, t + 1, pl.ds(margin + start, margin), :]
            k = (c * (tiles + 2) + t + 1) * margin
            a, b = ya_ref[k : k + margin, :].astype(f32), yb_ref[k : k + margin, :].astype(f32)
            above = jnp.where(lower_first, b, a)
            below = jnp.where(lower_first, a, b)
            value += jnp.where(first, above, 0.0) + jnp.where(last, below, 0.0)
            if t in (0, tiles - 1):
                rows = pl.ds(pl.multiple_of(c * tile_r + start, margin), margin)
                a, b = sa_ref[rows, :].astype(f32), sb_ref[rows, :].astype(f32)
                if t == 0:
                    value += jnp.where(right_first, b, a)
                if t == tiles - 1:
                    value += jnp.where(right_first, a, b)
            cols = slice(LANES * t, LANES * (t + 1))
            grad_ref[c, :, cols] = value
            out_ref[c, :, cols] = obj_ref[c, :, cols] - scale_ref[t, pl.ds(start, margin), :] * value


def on_device(object_field, probe, amplitudes, positions, counts):
    tile_r, tile_c = object_field.shape[1:]
    window = probe.shape[1]
    margin = window // 2
    batches, slots = amplitudes.shape[2:4]
    tiles = tile_c // LANES
    padded = (2, tiles + 2, tile_r + 2 * margin, LANES)
    real, imag = dft_parts(window)
    fwd = jnp.concatenate([jnp.concatenate([real, -imag], 1), jnp.concatenate([imag, real], 1)], 0)
    bwd = jnp.concatenate([jnp.concatenate([real, imag], 1), jnp.concatenate([-imag, real], 1)], 0)
    tables = jnp.stack([real, imag]).astype(f32)
    ext = jnp.concatenate([tables, tables], 1).reshape(2, 2 * window, 2, LANES).transpose(0, 2, 1, 3)
    places = positions.reshape(2 * batches * slots)
    lives = counts.reshape(batches)
    shape = jax.ShapeDtypeStruct
    side = shape((2 * tile_r + PACK, LANES), bf16)
    strip = shape((2 * (tiles + 2) * margin, LANES), bf16)

    za, zb = pl.pallas_call(
        edges_kernel,
        out_shape=(side, side),
        in_specs=[SMEM, SMEM, ANY],
        out_specs=(VMEM, VMEM),
        scratch_shapes=[pltpu.VMEM((2, tile_r, LANES), f32)] * 2 + [pltpu.SemaphoreType.DMA((2, 2))],
        name="edges",
    )(places, lives, object_field)
    za, zb = swap(za, "col", 0), swap(zb, "col", 1)
    obj, canvas = pl.pallas_call(
        prepare_kernel,
        out_shape=(shape(padded, f32), shape(padded, f32)),
        in_specs=[ANY],
        out_specs=(VMEM, VMEM),
        scratch_shapes=[pltpu.SemaphoreType.DMA((2, tiles))],
        compiler_params=pltpu.CompilerParams(vmem_limit_bytes=4 << 20),
        cost_estimate=pl.CostEstimate(flops=4 << 20, bytes_accessed=16 << 20, transcendentals=0),
        name="prepare",
    )(object_field)
    obj, ya, yb = pl.pallas_call(
        sides_kernel,
        out_shape=(shape(padded, f32), strip, strip),
        in_specs=[VMEM] * 3,
        out_specs=(VMEM,) * 3,
        input_output_aliases={0: 0},
        compiler_params=pltpu.CompilerParams(vmem_limit_bytes=4 << 20),
        name="sides",
    )(obj, za, zb)
    meta_own = jnp.zeros((1, LANES), bf16)
    from_left = jnp.where(even("col"), zb[2 * tile_r :], za[2 * tile_r :])
    from_right = jnp.where(even("col"), za[2 * tile_r :], zb[2 * tile_r :])
    shifted = places + LANES
    own = jnp.concatenate([shifted // 16, shifted % 16, lives, jnp.zeros((LANES - 51,), jnp.int32)])
    own = jnp.broadcast_to(own.astype(bf16)[None], (PACK, LANES))
    metas = jnp.concatenate([from_left, own, from_right], 0)
    ya, yb = jnp.concatenate([ya, metas], 0), jnp.concatenate([yb, metas], 0)
    ya, yb = swap(ya, "row", 0), swap(yb, "row", 1)
    tail = strip.shape[0]
    above = jnp.where(even("row"), yb[tail:], ya[tail:])
    below = jnp.where(even("row"), ya[tail:], yb[tail:])
    table = jnp.concatenate([above, metas, below], 0)[::PACK].astype(jnp.int32)

    _, canvas, ya, yb = pl.pallas_call(
        slots_kernel,
        out_shape=(shape(padded, f32), shape(padded, f32), strip, strip),
        in_specs=[SMEM, SMEM] + [VMEM] * 9,
        out_specs=(VMEM,) * 4,
        input_output_aliases={2: 0, 3: 1},
        scratch_shapes=[
            pltpu.SMEM((batches * slots,), jnp.int32),
            pltpu.VMEM((GROUP, 2, 2, window, LANES), f32),
            pltpu.VMEM((2 * window, GROUP * window), bf16),
            pltpu.VMEM((GROUP, window, 2 * window), bf16),
            pltpu.VMEM((GROUP, 2 * window, 2 * window), bf16),
        ],
        compiler_params=pltpu.CompilerParams(vmem_limit_bytes=14 << 20),
        name="slots",
    )(
        places, lives, obj, canvas, ya, yb, probe,
        amplitudes.reshape(batches * slots, window, window), fwd, bwd, ext,
    )
    ya, yb = swap(ya, "row", 0), swap(yb, "row", 1)
    scale = pl.pallas_call(
        light_kernel,
        out_shape=shape((tiles, tile_r, LANES), f32),
        in_specs=[SMEM, VMEM],
        out_specs=VMEM,
        scratch_shapes=[
            pltpu.VMEM((2, window, LANES), f32),
            pltpu.VMEM((tiles + 4, tile_r + 2 * window, LANES), f32),
        ],
        compiler_params=pltpu.CompilerParams(vmem_limit_bytes=9 << 20),
        cost_estimate=pl.CostEstimate(flops=8 << 20, bytes_accessed=12 << 20, transcendentals=0),
        name="light",
    )(table, probe)
    rim = shape((2 * tile_r, LANES), bf16)
    sa, sb = pl.pallas_call(
        strips_kernel,
        out_shape=(rim, rim),
        in_specs=[VMEM] * 3,
        out_specs=(VMEM, VMEM),
        compiler_params=pltpu.CompilerParams(vmem_limit_bytes=4 << 20),
        name="strips",
    )(canvas, ya, yb)
    sa, sb = swap(sa, "col", 0), swap(sb, "col", 1)
    block = pl.BlockSpec((2, margin, tile_c), lambda i: (0, i, 0))
    field = shape((2, tile_r, tile_c), f32)
    return pl.pallas_call(
        update_kernel,
        grid=(tile_r // margin,),
        out_shape=(field, field),
        in_specs=[block] + [VMEM] * 6,
        out_specs=(block, block),
        compiler_params=pltpu.CompilerParams(vmem_limit_bytes=8 << 20),
        name="update",
    )(object_field, canvas, ya, yb, sa, sb, scale)


def solution(mesh):
    in_specs = (
        P(None, "row", "col"),
        P(),
        P("row", "col", None, None, None, None),
        P("row", "col", None, None, None),
        P("row", "col", None),
    )
    out_specs = (P(None, "row", "col"), P(None, "row", "col"))
    return jax.shard_map(
        on_device, mesh=mesh, in_specs=in_specs, out_specs=out_specs, check_vma=False
    )
```

profile of v0, /device:TPU:34, one launch (start us, length us, event | category | flops | bytes accessed | tf_op | source)
XLA Modules:
  0.0 84.6 jit_solution(11715254768190142402)
XLA Ops:
  0.6 0.8 copy.11
  1.4 0.6 reshape.132.pos_ref
  2.0 3.0 %edges.1 = (bf16[1552,128]{1,0:T(8,128)(2,1)}, bf16[1552,128]{1,0:T(8,128)(2,1)}) custom-call(s32[24]{0:T(128)} %reshape.132.pos_ref, s32[3]{0:T(128)} %bitcast.6, f32[2,768,512]{2,1,0:T(8,128)} %obj_ref.1), custom_call_target="tpu_custom_call" | custom-call | tf_op jit(solution)/shard_map/edges/pallas_call | solution.py:385
  5.3 5.6 %collective-permute-start.1 = (bf16[1552,128]{1,0:T(8,128)(2,1)}, bf16[1552,128]{1,0:T(8,128)(2,1)S(1)}, u32[]{:S(2)}, u32[]{:S(2)}) collective-permute-start(bf16[1552,128]{1,0:T(8,128)(2,1)} %get-tuple-element.16), channel_id=1, source_target_pairs={{1,2},{2,1},{3,4},{4,3},{5,6},{6,5},{9,10},{10,9},{11,12},{12,11},... | collective-permute-start | bytes 1191944 | tf_op jit(solution)/shard_map/ppermute | solution.py:27
  10.9 0.7 bitcast_convert_fusion
  11.6 0.6 fusion.16
  12.3 1.9 %copy-done.3 = f32[2,768,512]{2,1,0:T(8,128)S(1)} copy-done((f32[2,768,512]{2,1,0:T(8,128)S(1)}, f32[2,768,512]{2,1,0:T(8,128)}, u32[]{:S(2)}) %copy-start.3) | copy-done | bytes 3145752
  14.2 1.1 %prepare.1 = (f32[2,6,1024,128]{3,2,1,0:T(8,128)S(1)}, f32[2,6,1024,128]{3,2,1,0:T(8,128)S(1)}) custom-call(f32[2,768,512]{2,1,0:T(8,128)S(1)} %copy-done.3), custom_call_target="tpu_custom_call" | custom-call | flops 4194304 | bytes 16777216 | tf_op jit(solution)/shard_map/prepare/pallas_call | solution.py:394
  15.4 1.1 %multiply_convert_fusion.1 = (bf16[1,256,2,128]{3,1,2,0:T(8,128)(2,1)S(1)}, bf16[1,256,2,128]{3,1,2,0:T(8,128)(2,1)S(1)}) fusion(s32[2,128]{1,0:T(2,128)S(1)} %multiply_add_fusion), kind=kLoop, calls=%fused_computation.26 | loop fusion | flops 1245184 | bytes 263168 | tf_op jit(solution)/shard_map/convert_element_type | solution.py:40
  16.6 3.5 %collective-permute-done.1.zb_ref = bf16[1552,128]{1,0:T(8,128)(2,1)S(1)} collective-permute-done((bf16[1552,128]{1,0:T(8,128)(2,1)}, bf16[1552,128]{1,0:T(8,128)(2,1)S(1)}, u32[]{:S(2)}, u32[]{:S(2)}) %collective-permute-start.1) | collective-permute-done | bytes 397344 | tf_op jit(solution)/shard_map/ppermute | solution.py:27
  20.3 3.5 %collective-permute-start.3 = (bf16[1584,128]{1,0:T(8,128)(2,1)S(1)}, bf16[1584,128]{1,0:T(8,128)(2,1)S(1)}, u32[]{:S(2)}, u32[]{:S(2)}) collective-permute-start(bf16[1584,128]{1,0:T(8,128)(2,1)S(1)} %get-tuple-element.32), channel_id=1, source_target_pairs={{8,16},{16,8},{24,32},{32,24},{40,48},{48,40},{56,64},{64,56},{72,... | collective-permute-start | bytes 1216520 | tf_op jit(solution)/shard_map/ppermute | solution.py:27
  23.8 0.2 collective-permute-start.2
  24.0 1.0 %fusion.14 = bf16[256,256]{1,0:T(8,128)(2,1)S(1)} fusion(), kind=kLoop, calls=%fused_computation.35 | loop fusion | flops 1310720 | bytes 131072 | tf_op jit(solution)/shard_map/neg | solution.py:375
  25.0 1.1 %multiply_convert_fusion.2 = (bf16[256,256]{1,0:T(8,128)(2,1)S(1)}, bf16[256,256]{1,0:T(8,128)(2,1)S(1)}) fusion(), kind=kLoop, calls=%fused_computation.29 | loop fusion | flops 1245184 | bytes 262144 | tf_op jit(solution)/shard_map/convert_element_type | solution.py:41
  26.3 5.4 %collective-permute-done.3.yb_ref = bf16[1584,128]{1,0:T(8,128)(2,1)S(1)} collective-permute-done((bf16[1584,128]{1,0:T(8,128)(2,1)S(1)}, bf16[1584,128]{1,0:T(8,128)(2,1)S(1)}, u32[]{:S(2)}, u32[]{:S(2)}) %collective-permute-start.3) | collective-permute-done | bytes 405536 | tf_op jit(solution)/shard_map/ppermute | solution.py:27
  31.7 6.9 %slots.1 = (f32[2,6,1024,128]{3,2,1,0:T(8,128)S(1)}, f32[2,6,1024,128]{3,2,1,0:T(8,128)S(1)}, bf16[1536,128]{1,0:T(8,128)(2,1)}, bf16[1536,128]{1,0:T(8,128)(2,1)}) custom-call(s32[24]{0:T(128)S(1)} %copy-done.10, s32[3]{0:T(128)S(1)} %bitcast.7, f32[2,6,1024,128]{3,2,1,0:T(8,128)S(1)} %get-tuple-element.17.obj_in, ...), custom_call_target="tpu_custom_call", output_to_operand_aliasing={{0}: (2, {}), {1}: (3, {})} | custom-call | tf_op jit(solution)/shard_map/slots/pallas_call | solution.py:427
  38.7 2.6 %copy-done = f32[2,6,1024,128]{3,2,1,0:T(8,128)} copy-done((f32[2,6,1024,128]{3,2,1,0:T(8,128)}, f32[2,6,1024,128]{3,2,1,0:T(8,128)S(1)}, u32[]{:S(2)}) %copy-start) | copy-done | bytes 6291480
  41.3 3.4 %collective-permute-start.5 = (bf16[1536,128]{1,0:T(8,128)(2,1)}, bf16[1536,128]{1,0:T(8,128)(2,1)}, u32[]{:S(2)}, u32[]{:S(2)}) collective-permute-start(bf16[1536,128]{1,0:T(8,128)(2,1)} %get-tuple-element.23), channel_id=1, source_target_pairs={{8,16},{16,8},{24,32},{32,24},{40,48},{48,40},{56,64},{64,56},{72,... | collective-permute-start | bytes 1179656 | tf_op jit(solution)/shard_map/ppermute | solution.py:27
  44.7 1.3 %select_dynamic-update-slice_fusion.1 = bf16[144,128]{1,0:T(8,128)(2,1)} fusion(pred[]{:T(512)S(6)} %eq.13, bf16[1584,128]{1,0:T(8,128)(2,1)} %copy-done.9, bf16[1584,128]{1,0:T(8,128)(2,1)} %copy-done.8), kind=kLoop, calls=%fused_computation.37 | loop fusion | flops 6143 | bytes 36865
  46.1 0.6 constant_dynamic-update-slice_fusion.2
  46.7 6.1 %collective-permute-done.5.yb_ref = bf16[1536,128]{1,0:T(8,128)(2,1)} collective-permute-done((bf16[1536,128]{1,0:T(8,128)(2,1)}, bf16[1536,128]{1,0:T(8,128)(2,1)}, u32[]{:S(2)}, u32[]{:S(2)}) %collective-permute-start.5) | collective-permute-done | bytes 393248 | tf_op jit(solution)/shard_map/ppermute | solution.py:27
  52.8 2.8 %copy-done.1 = f32[2,6,1024,128]{3,2,1,0:T(8,128)S(1)} copy-done((f32[2,6,1024,128]{3,2,1,0:T(8,128)S(1)}, f32[2,6,1024,128]{3,2,1,0:T(8,128)}, u32[]{:S(2)}) %copy-start.1) | copy-done | bytes 6291480
  55.6 2.1 %strips.1 = (bf16[1536,128]{1,0:T(8,128)(2,1)}, bf16[1536,128]{1,0:T(8,128)(2,1)}) custom-call(f32[2,6,1024,128]{3,2,1,0:T(8,128)S(1)} %copy-done.1, bf16[1536,128]{1,0:T(8,128)(2,1)S(1)} %collective-permute-done.4.ya_ref, bf16[1536,128]{1,0:T(8,128)(2,1)} %collective-permute-done.5.yb_ref), custom_call_target="tpu_custom_call" | custom-call | tf_op jit(solution)/shard_map/strips/pallas_call | solution.py:461
  57.7 7.8 %collective-permute-start.7 = (bf16[1536,128]{1,0:T(8,128)(2,1)}, bf16[1536,128]{1,0:T(8,128)(2,1)}, u32[]{:S(2)}, u32[]{:S(2)}) collective-permute-start(bf16[1536,128]{1,0:T(8,128)(2,1)} %get-tuple-element.25), channel_id=1, source_target_pairs={{1,2},{2,1},{3,4},{4,3},{5,6},{6,5},{9,10},{10,9},{11,12},{12,11},... | collective-permute-start | bytes 1179656 | tf_op jit(solution)/shard_map/ppermute | solution.py:27
  65.5 0.6 constant_dynamic-update-slice_fusion.1
  66.1 0.6 constant_dynamic-update-slice_fusion
  66.7 1.3 %select_dynamic-update-slice_fusion = bf16[144,128]{1,0:T(8,128)(2,1)} fusion(bf16[144,128]{1,0:T(8,128)(2,1)} %constant_dynamic-update-slice_fusion, pred[]{:T(512)S(6)} %eq.13, bf16[1584,128]{1,0:T(8,128)(2,1)} %copy-done.9, bf16[1584,128]{1,0:T(8,128)(2,1)} %copy-done.8), kind=kLoop, calls=%fused_computation.36 | loop fusion | flops 6144 | bytes 36865 | tf_op jit(solution)/shard_map/concatenate | solution.py:425
  68.0 0.8 slice.23
  68.8 1.0 %copy-done.6 = f32[2,256,256]{2,1,0:T(8,128)S(1)} copy-done((f32[2,256,256]{2,1,0:T(8,128)S(1)}, f32[2,256,256]{2,1,0:T(8,128)}, u32[]{:S(2)}) %copy-start.6) | copy-done | bytes 524312
  69.8 6.7 %light.1.scale_ref = f32[4,768,128]{2,1,0:T(8,128)S(1)} custom-call(s32[9,128]{1,0:T(8,128)S(1)} %convert_element_type.89.meta_ref, f32[2,256,256]{2,1,0:T(8,128)S(1)} %copy-done.6), custom_call_target="tpu_custom_call" | custom-call | flops 8388608 | bytes 12582912 | tf_op jit(solution)/shard_map/light/pallas_call | solution.py:447
  76.6 2.8 %copy-done.2 = f32[2,6,1024,128]{3,2,1,0:T(8,128)S(1)} copy-done((f32[2,6,1024,128]{3,2,1,0:T(8,128)S(1)}, f32[2,6,1024,128]{3,2,1,0:T(8,128)}, u32[]{:S(2)}) %copy-start.2) | copy-done | bytes 6291480
  79.3 5.3 %update.1 = (f32[2,768,512]{2,1,0:T(8,128)}, f32[2,768,512]{2,1,0:T(8,128)}) custom-call(f32[2,768,512]{2,1,0:T(8,128)S(1)} %copy-done.4, f32[2,6,1024,128]{3,2,1,0:T(8,128)S(1)} %copy-done.2, bf16[1536,128]{1,0:T(8,128)(2,1)S(1)} %collective-permute-done.4.ya_ref, bf16[1536,128]{1,0:T(8,128)(2,1)} %collective-permute-done.5.yb_ref, ...), custom_call_target="tpu_custom_call" | custom-call | tf_op jit(solution)/shard_map/update/pallas_call | solution.py:472
  (38 shorter events, 0.8 us)
Async XLA Ops:
  5.1 11.5 %collective-permute-start = (bf16[1552,128]{1,0:T(8,128)(2,1)}, bf16[1552,128]{1,0:T(8,128)(2,1)S(1)}, u32[]{:S(2)}, u32[]{:S(2)}) collective-permute-start(bf16[1552,128]{1,0:T(8,128)(2,1)} %get-tuple-element.15), channel_id=1, source_target_pairs={{0,1},{1,0},{2,3},{3,2},{4,5},{5,4},{6,7},{7,6},{8,9},{9,8},{10,11... | collective-permute-start | bytes 1191944 | tf_op jit(solution)/shard_map/ppermute | solution.py:27
  5.3 14.7 %collective-permute-start.1 = (bf16[1552,128]{1,0:T(8,128)(2,1)}, bf16[1552,128]{1,0:T(8,128)(2,1)S(1)}, u32[]{:S(2)}, u32[]{:S(2)}) collective-permute-start(bf16[1552,128]{1,0:T(8,128)(2,1)} %get-tuple-element.16), channel_id=1, source_target_pairs={{1,2},{2,1},{3,4},{4,3},{5,6},{6,5},{9,10},{10,9},{11,12},{12,11},... | collective-permute-start | bytes 1191944 | tf_op jit(solution)/shard_map/ppermute | solution.py:27
  12.3 1.9 %copy-start.3 = (f32[2,768,512]{2,1,0:T(8,128)S(1)}, f32[2,768,512]{2,1,0:T(8,128)}, u32[]{:S(2)}) copy-start(f32[2,768,512]{2,1,0:T(8,128)} %obj_ref.1) | copy-start | bytes 9437188
  15.4 16.3 %copy-start.5 = (f32[2,256,256]{2,1,0:T(8,128)S(1)}, f32[2,256,256]{2,1,0:T(8,128)}, u32[]{:S(2)}) copy-start(f32[2,256,256]{2,1,0:T(8,128)} %probe_ref.3) | copy-start | bytes 1572868
  15.4 16.3 %copy-start.7 = (bf16[1,1,3,4,256,256]{5,4,3,2,1,0:T(8,128)(2,1)S(1)}, bf16[1,1,3,4,256,256]{5,4,3,2,1,0:T(8,128)(2,1)}, u32[]{:S(2)}) copy-start(bf16[1,1,3,4,256,256]{5,4,3,2,1,0:T(8,128)(2,1)} %param.7) | copy-start | bytes 4718596
  15.4 16.3 %copy-start.10 = (s32[24]{0:T(128)S(1)}, s32[24]{0:T(128)}, u32[]{:S(2)}) copy-start(s32[24]{0:T(128)} %reshape.132.pos_ref) | copy-start | bytes 292
  15.4 16.3 %copy-start.11 = (s32[1,1,3]{2,1,0:T(1,128)S(1)}, s32[1,1,3]{2,1,0:T(1,128)}, u32[]{:S(2)}) copy-start(s32[1,1,3]{2,1,0:T(1,128)} %param.9) | copy-start | bytes 40
  20.3 11.3 %collective-permute-start.3 = (bf16[1584,128]{1,0:T(8,128)(2,1)S(1)}, bf16[1584,128]{1,0:T(8,128)(2,1)S(1)}, u32[]{:S(2)}, u32[]{:S(2)}) collective-permute-start(bf16[1584,128]{1,0:T(8,128)(2,1)S(1)} %get-tuple-element.32), channel_id=1, source_target_pairs={{8,16},{16,8},{24,32},{32,24},{40,48},{48,40},{56,64},{64,56},{72,... | collective-permute-start | bytes 1216520 | tf_op jit(solution)/shard_map/ppermute | solution.py:27
  23.8 7.9 %collective-permute-start.2 = (bf16[1584,128]{1,0:T(8,128)(2,1)S(1)}, bf16[1584,128]{1,0:T(8,128)(2,1)S(1)}, u32[]{:S(2)}, u32[]{:S(2)}) collective-permute-start(bf16[1584,128]{1,0:T(8,128)(2,1)S(1)} %get-tuple-element.33), channel_id=1, source_target_pairs={{0,8},{8,0},{16,24},{24,16},{32,40},{40,32},{48,56},{56,48},{64,72... | collective-permute-start | bytes 1216520 | tf_op jit(solution)/shard_map/ppermute | solution.py:27
  31.7 7.0 %copy-start.8 = (bf16[1584,128]{1,0:T(8,128)(2,1)}, bf16[1584,128]{1,0:T(8,128)(2,1)S(1)}, u32[]{:S(2)}) copy-start(bf16[1584,128]{1,0:T(8,128)(2,1)S(1)} %collective-permute-done.3.yb_ref) | copy-start | bytes 1216516
  31.7 7.0 %copy-start.9 = (bf16[1584,128]{1,0:T(8,128)(2,1)}, bf16[1584,128]{1,0:T(8,128)(2,1)S(1)}, u32[]{:S(2)}) copy-start(bf16[1584,128]{1,0:T(8,128)(2,1)S(1)} %collective-permute-done.2.ya_ref) | copy-start | bytes 1216516
  31.7 44.8 %copy-start.4 = (f32[2,768,512]{2,1,0:T(8,128)S(1)}, f32[2,768,512]{2,1,0:T(8,128)}, u32[]{:S(2)}) copy-start(f32[2,768,512]{2,1,0:T(8,128)} %obj_ref.1) | copy-start | bytes 9437188
  38.7 2.6 %copy-start = (f32[2,6,1024,128]{3,2,1,0:T(8,128)}, f32[2,6,1024,128]{3,2,1,0:T(8,128)S(1)}, u32[]{:S(2)}) copy-start(f32[2,6,1024,128]{3,2,1,0:T(8,128)S(1)} %get-tuple-element.21.canvas_ref) | copy-start | bytes 18874372
  41.3 5.4 %collective-permute-start.4 = (bf16[1536,128]{1,0:T(8,128)(2,1)}, bf16[1536,128]{1,0:T(8,128)(2,1)S(1)}, u32[]{:S(2)}, u32[]{:S(2)}) collective-permute-start(bf16[1536,128]{1,0:T(8,128)(2,1)} %get-tuple-element.22), channel_id=1, source_target_pairs={{0,8},{8,0},{16,24},{24,16},{32,40},{40,32},{48,56},{56,48},{64,72... | collective-permute-start | bytes 1179656 | tf_op jit(solution)/shard_map/ppermute | solution.py:27
  41.3 11.5 %collective-permute-start.5 = (bf16[1536,128]{1,0:T(8,128)(2,1)}, bf16[1536,128]{1,0:T(8,128)(2,1)}, u32[]{:S(2)}, u32[]{:S(2)}) collective-permute-start(bf16[1536,128]{1,0:T(8,128)(2,1)} %get-tuple-element.23), channel_id=1, source_target_pairs={{8,16},{16,8},{24,32},{32,24},{40,48},{48,40},{56,64},{64,56},{72,... | collective-permute-start | bytes 1179656 | tf_op jit(solution)/shard_map/ppermute | solution.py:27
  52.8 2.8 %copy-start.1 = (f32[2,6,1024,128]{3,2,1,0:T(8,128)S(1)}, f32[2,6,1024,128]{3,2,1,0:T(8,128)}, u32[]{:S(2)}) copy-start(f32[2,6,1024,128]{3,2,1,0:T(8,128)} %copy-done) | copy-start | bytes 18874372
  57.7 18.8 %collective-permute-start.6 = (bf16[1536,128]{1,0:T(8,128)(2,1)}, bf16[1536,128]{1,0:T(8,128)(2,1)}, u32[]{:S(2)}, u32[]{:S(2)}) collective-permute-start(bf16[1536,128]{1,0:T(8,128)(2,1)} %get-tuple-element.24), channel_id=1, source_target_pairs={{0,1},{1,0},{2,3},{3,2},{4,5},{5,4},{6,7},{7,6},{8,9},{9,8},{10,11... | collective-permute-start | bytes 1179656 | tf_op jit(solution)/shard_map/ppermute | solution.py:27
  57.7 18.8 %collective-permute-start.7 = (bf16[1536,128]{1,0:T(8,128)(2,1)}, bf16[1536,128]{1,0:T(8,128)(2,1)}, u32[]{:S(2)}, u32[]{:S(2)}) collective-permute-start(bf16[1536,128]{1,0:T(8,128)(2,1)} %get-tuple-element.25), channel_id=1, source_target_pairs={{1,2},{2,1},{3,4},{4,3},{5,6},{6,5},{9,10},{10,9},{11,12},{12,11},... | collective-permute-start | bytes 1179656 | tf_op jit(solution)/shard_map/ppermute | solution.py:27
  68.8 1.0 %copy-start.6 = (f32[2,256,256]{2,1,0:T(8,128)S(1)}, f32[2,256,256]{2,1,0:T(8,128)}, u32[]{:S(2)}) copy-start(f32[2,256,256]{2,1,0:T(8,128)} %probe_ref.3) | copy-start | bytes 1572868
  76.5 2.8 %copy-start.2 = (f32[2,6,1024,128]{3,2,1,0:T(8,128)S(1)}, f32[2,6,1024,128]{3,2,1,0:T(8,128)}, u32[]{:S(2)}) copy-start(f32[2,6,1024,128]{3,2,1,0:T(8,128)} %copy-done) | copy-start | bytes 18874372
where the time goes:
time: 84.5 us; the launch traced here: 84.6 us
  Pallas kernels  25.4 us (30%)
  starting transfers between devices  20.7 us (24%)
  local copies, waits for them, and re-layouts  15.1 us (18%)
  waiting for transfers between devices  15 us (18%)
  other arithmetic  7.52 us (9%)
  between operations  0.89 us (1%)
    ppermute x8, starting transfers between devices, swap(): return lax.ppermute(block, axis, route)  20.7 us
    ppermute x8, waiting for transfers between devices, swap(): return lax.ppermute(block, axis, route)  15 us
    unnamed x28, local copies, waits for them, and re-layouts  13.7 us
    pallas_call x1, Pallas kernels, on_device(): pl.pallas_call(slots_kernel, out_shape=(shape(padded, f32), shape(padded,...  6.93 us
    pallas_call x1, Pallas kernels, on_device(): pl.pallas_call(light_kernel, out_shape=shape((tiles, tile_r, LANES), f32)...  6.68 us
    pallas_call x1, Pallas kernels, on_device(): pl.pallas_call(update_kernel, grid=(tile_r // margin,), out_shape=(field,...  5.3 us
    pallas_call x1, Pallas kernels, on_device(): pl.pallas_call(edges_kernel, out_shape=(side, side), in_specs=[SMEM, SMEM...  3.03 us
    pallas_call x1, Pallas kernels, on_device(): pl.pallas_call(strips_kernel, out_shape=(rim, rim), in_specs=[VMEM] * 3,...  2.11 us
  transfers between devices with their start and end apart: 8, of which 3 were waited for; matrix products, arithmetic and copies ran while one was open for 12% of the time, Pallas kernels for 9%

commit v1 on v0

--- a/solution.py
+++ b/solution.py
@@ -1,3 +1,4 @@
+import functools
 import math
 
 import jax
@@ -101,7 +102,7 @@
         obj_ref[c, t + 1, body, :] = obj_ref[c, t + 1, body, :].astype(bf16).astype(f32)
 
 
-def sides_kernel(obj_in, za_ref, zb_ref, obj_ref, ya_ref, yb_ref):
+def sides_kernel(obj_in, za_ref, zb_ref, own_ref, obj_ref, ya_ref, yb_ref, meta_ref):
     tiles = obj_ref.shape[1] - 2
     margin = LANES
     tile_r = obj_ref.shape[2] - 2 * margin
@@ -122,13 +123,24 @@
             k = (c * (tiles + 2) + t) * margin
             ya_ref[k : k + margin, :] = jnp.where(downward, bottom, top).astype(bf16)
             yb_ref[k : k + margin, :] = jnp.where(downward, top, bottom).astype(bf16)
-
-
-def slots_kernel(
-    pos_ref, counts_ref, obj_in, canvas_in, ya_ref, yb_ref, probe_ref, amp_ref, fwd_ref, bwd_ref, ext_ref,
-    obj, canvas_ref, ra_ref, rb_ref,
-    todo, prb, xs, hs, er,
-):
+    tail = 2 * (tiles + 2) * margin
+    a = za_ref[2 * tile_r :, :].astype(f32)
+    b = zb_ref[2 * tile_r :, :].astype(f32)
+    metas = (jnp.where(right_first, b, a).astype(bf16), own_ref[2 * tile_r :, :], jnp.where(right_first, a, b).astype(bf16))
+    for k, meta in enumerate(metas):
+        rows = slice(tail + PACK * k, tail + PACK * (k + 1))
+        ya_ref[rows, :] = meta
+        yb_ref[rows, :] = meta
+        meta_ref[PACK * k : PACK * (k + 1), :] = meta
+
+
+def slots_kernel(outer, *refs):
+    if outer:
+        (pos_ref, counts_ref, obj_in, canvas_in, ya_ref, yb_ref, probe_ref, amp_ref, fwd_ref, bwd_ref, ext_ref,
+         obj, canvas_ref, ra_ref, rb_ref, todo, prb, xs, hs, er) = refs
+    else:
+        (pos_ref, counts_ref, obj, canvas_in, probe_ref, amp_ref, fwd_ref, bwd_ref, ext_ref,
+         canvas_ref, todo, prb, xs, hs, er) = refs
     batches = counts_ref.shape[0]
     slots = pos_ref.shape[0] // (2 * batches)
     win = probe_ref.shape[1]
@@ -136,7 +148,7 @@
     tiles = obj.shape[1] - 2
     tile_r = obj.shape[2] - 2 * margin
     lower_first = even("row")
-    for c in range(2):
+    for c in range(2 if outer else 0):
         for t in range(tiles + 2):
             k = (c * (tiles + 2) + t) * margin
             a = ya_ref[k : k + margin, :].astype(f32)
@@ -146,7 +158,9 @@
 
     def collect(slot, count):
         batch = slot // slots
-        live = slot - batch * slots < counts_ref[batch]
+        row = pos_ref[2 * slot]
+        inside = (row >= 0) & (row <= tile_r - win)
+        live = (slot - batch * slots < counts_ref[batch]) & (inside != outer)
 
         @pl.when(live)
         def _():
@@ -254,7 +268,7 @@
 
     lax.fori_loop(0, (total + GROUP - 1) // GROUP, group, 0)
 
-    for c in range(2):
+    for c in range(2 if outer else 0):
         for t in range(tiles + 2):
             k = (c * (tiles + 2) + t) * margin
             top = canvas_ref[c, t, 0:margin, :]
@@ -263,38 +277,47 @@
             rb_ref[k : k + margin, :] = jnp.where(lower_first, top, bottom).astype(bf16)
 
 
-def light_kernel(meta_ref, probe_ref, scale_ref, power, light):
+def light_kernel(meta_ref, ya_ref, yb_ref, probe_ref, scale_ref, power, light, rows_ref, table_ref, sem):
     win = probe_ref.shape[1]
     tiles, tile_r = scale_ref.shape[:2]
     tile_c = tiles * LANES
-    fields = 51
     batches = 3
     slots = 4
-    light[...] = jnp.zeros_like(light)
+    step = 2 * batches * slots
+    lower_first = even("row")
+    tail = ya_ref.shape[0] - 3 * PACK
+    for k in range(3):
+        rows = slice(tail + PACK * k, tail + PACK * (k + 1))
+        a, b = ya_ref[rows, :].astype(f32), yb_ref[rows, :].astype(f32)
+        rows_ref[k : k + 1, :] = jnp.where(lower_first, b, a)[0:1].astype(jnp.int32)
+        rows_ref[3 + k : 4 + k, :] = meta_ref[PACK * k : PACK * (k + 1), :].astype(f32)[0:1].astype(jnp.int32)
+        rows_ref[6 + k : 7 + k, :] = jnp.where(lower_first, a, b)[0:1].astype(jnp.int32)
+    copy = pltpu.make_async_copy(rows_ref, table_ref, sem)
+    copy.start()
+    for t in range(tiles + 4):
+        light[t] = jnp.zeros_like(light[t])
     for h in range(2):
         cols = slice(LANES * h, LANES * (h + 1))
         real, imag = probe_ref[0, :, cols], probe_ref[1, :, cols]
         power[h] = real * real + imag * imag
-    step = 2 * batches * slots
+    copy.wait()
 
     def tile_slots(n, carry):
         down = n // 3 - 1
         across = n - (down + 1) * 3 - 1
 
         def one(slot, inner):
-            batch = slot // slots
-            row = meta_ref[n, 2 * slot] * 16 + meta_ref[n, step + 2 * slot] - LANES + down * tile_r
-            col = meta_ref[n, 2 * slot + 1] * 16 + meta_ref[n, step + 2 * slot + 1] - LANES + across * tile_c
-            live = slot - batch * slots < meta_ref[n, 2 * step + batch]
+            row = table_ref[n, 2 * slot] * 16 + table_ref[n, step + 2 * slot] - LANES + down * tile_r
+            col = table_ref[n, 2 * slot + 1] * 16 + table_ref[n, step + 2 * slot + 1] - LANES + across * tile_c
             meets = (row > -win) & (row < tile_r) & (col > -win) & (col < tile_c)
 
-            @pl.when(live & meets)
+            @pl.when(meets)
             def _():
                 place = col + win
                 tile = place // LANES
                 shift = place - tile * LANES
+                low = lax.broadcasted_iota(jnp.int32, (64, LANES), 1) < shift
                 for i in range(0, win, 64):
-                    low = lax.broadcasted_iota(jnp.int32, (64, LANES), 1) < shift
                     one_half = pltpu.roll(power[0, i : i + 64, :], shift, 1)
                     two_half = pltpu.roll(power[1, i : i + 64, :], shift, 1)
                     at = pl.ds(row + win + i, 64)
@@ -304,7 +327,9 @@
 
             return inner
 
-        return lax.fori_loop(0, batches * slots, one, carry)
+        for batch in range(batches):
+            carry = lax.fori_loop(slots * batch, slots * batch + table_ref[n, 2 * step + batch], one, carry)
+        return carry
 
     lax.fori_loop(0, 9, tile_slots, 0)
     for t in range(tiles):
@@ -344,24 +369,32 @@
     first = step == 0
     last = step == pl.num_programs(0) - 1
     start = pl.multiple_of(step * margin, margin)
-    for c in range(2):
-        for t in range(tiles):
-            value = canvas_ref[c, t + 1, pl.ds(margin + start, margin), :]
-            k = (c * (tiles + 2) + t + 1) * margin
-            a, b = ya_ref[k : k + margin, :].astype(f32), yb_ref[k : k + margin, :].astype(f32)
-            above = jnp.where(lower_first, b, a)
-            below = jnp.where(lower_first, a, b)
-            value += jnp.where(first, above, 0.0) + jnp.where(last, below, 0.0)
-            if t in (0, tiles - 1):
-                rows = pl.ds(pl.multiple_of(c * tile_r + start, margin), margin)
-                a, b = sa_ref[rows, :].astype(f32), sb_ref[rows, :].astype(f32)
-                if t == 0:
-                    value += jnp.where(right_first, b, a)
-                if t == tiles - 1:
-                    value += jnp.where(right_first, a, b)
-            cols = slice(LANES * t, LANES * (t + 1))
-            grad_ref[c, :, cols] = value
-            out_ref[c, :, cols] = obj_ref[c, :, cols] - scale_ref[t, pl.ds(start, margin), :] * value
+    def write(edge):
+        for c in range(2):
+            for t in range(tiles):
+                value = canvas_ref[c, t + 1, pl.ds(margin + start, margin), :]
+                if edge:
+                    k = (c * (tiles + 2) + t + 1) * margin
+                    a, b = ya_ref[k : k + margin, :].astype(f32), yb_ref[k : k + margin, :].astype(f32)
+                    value += jnp.where(lower_first == first, b, a)
+                if t in (0, tiles - 1):
+                    rows = pl.ds(pl.multiple_of(c * tile_r + start, margin), margin)
+                    a, b = sa_ref[rows, :].astype(f32), sb_ref[rows, :].astype(f32)
+                    if t == 0:
+                        value += jnp.where(right_first, b, a)
+                    if t == tiles - 1:
+                        value += jnp.where(right_first, a, b)
+                cols = slice(LANES * t, LANES * (t + 1))
+                grad_ref[c, :, cols] = value
+                out_ref[c, :, cols] = obj_ref[c, :, cols] - scale_ref[t, pl.ds(start, margin), :] * value
+
+    @pl.when(first | last)
+    def _():
+        write(True)
+
+    @pl.when(jnp.logical_not(first | last))
+    def _():
+        write(False)
 
 
 def on_device(object_field, probe, amplitudes, positions, counts):
@@ -390,6 +423,7 @@
         scratch_shapes=[pltpu.VMEM((2, tile_r, LANES), f32)] * 2 + [pltpu.SemaphoreType.DMA((2, 2))],
         name="edges",
     )(places, lives, object_field)
+    own = za
     za, zb = swap(za, "col", 0), swap(zb, "col", 1)
     obj, canvas = pl.pallas_call(
         prepare_kernel,
@@ -401,62 +435,66 @@
         cost_estimate=pl.CostEstimate(flops=4 << 20, bytes_accessed=16 << 20, transcendentals=0),
         name="prepare",
     )(object_field)
-    obj, ya, yb = pl.pallas_call(
+    obj, fwd, bwd, ext = lax.optimization_barrier((obj, fwd, bwd, ext))
+    packed = shape((strip.shape[0] + 3 * PACK, LANES), bf16)
+    obj, ya, yb, meta = pl.pallas_call(
         sides_kernel,
-        out_shape=(shape(padded, f32), strip, strip),
-        in_specs=[VMEM] * 3,
-        out_specs=(VMEM,) * 3,
+        out_shape=(shape(padded, f32), packed, packed, shape((3 * PACK, LANES), bf16)),
+        in_specs=[VMEM] * 4,
+        out_specs=(VMEM,) * 4,
         input_output_aliases={0: 0},
         compiler_params=pltpu.CompilerParams(vmem_limit_bytes=4 << 20),
         name="sides",
-    )(obj, za, zb)
-    meta_own = jnp.zeros((1, LANES), bf16)
-    from_left = jnp.where(even("col"), zb[2 * tile_r :], za[2 * tile_r :])
-    from_right = jnp.where(even("col"), za[2 * tile_r :], zb[2 * tile_r :])
-    shifted = places + LANES
-    own = jnp.concatenate([shifted // 16, shifted % 16, lives, jnp.zeros((LANES - 51,), jnp.int32)])
-    own = jnp.broadcast_to(own.astype(bf16)[None], (PACK, LANES))
-    metas = jnp.concatenate([from_left, own, from_right], 0)
-    ya, yb = jnp.concatenate([ya, metas], 0), jnp.concatenate([yb, metas], 0)
+    )(obj, za, zb, own)
     ya, yb = swap(ya, "row", 0), swap(yb, "row", 1)
-    tail = strip.shape[0]
-    above = jnp.where(even("row"), yb[tail:], ya[tail:])
-    below = jnp.where(even("row"), ya[tail:], yb[tail:])
-    table = jnp.concatenate([above, metas, below], 0)[::PACK].astype(jnp.int32)
-
-    _, canvas, ya, yb = pl.pallas_call(
-        slots_kernel,
+    amps = amplitudes.reshape(batches * slots, window, window)
+    scratch = [
+        pltpu.SMEM((batches * slots,), jnp.int32),
+        pltpu.VMEM((GROUP, 2, 2, window, LANES), f32),
+        pltpu.VMEM((2 * window, GROUP * window), bf16),
+        pltpu.VMEM((GROUP, window, 2 * window), bf16),
+        pltpu.VMEM((GROUP, 2 * window, 2 * window), bf16),
+    ]
+    canvas = pl.pallas_call(
+        functools.partial(slots_kernel, False),
+        out_shape=shape(padded, f32),
+        in_specs=[SMEM, SMEM] + [VMEM] * 7,
+        out_specs=VMEM,
+        input_output_aliases={3: 0},
+        scratch_shapes=scratch,
+        compiler_params=pltpu.CompilerParams(vmem_limit_bytes=14 << 20),
+        cost_estimate=pl.CostEstimate(flops=4 << 30, bytes_accessed=20 << 20, transcendentals=0),
+        name="inner",
+    )(places, lives, obj, canvas, probe, amps, fwd, bwd, ext)
+    _, canvas, ra, rb = pl.pallas_call(
+        functools.partial(slots_kernel, True),
         out_shape=(shape(padded, f32), shape(padded, f32), strip, strip),
         in_specs=[SMEM, SMEM] + [VMEM] * 9,
         out_specs=(VMEM,) * 4,
         input_output_aliases={2: 0, 3: 1},
-        scratch_shapes=[
-            pltpu.SMEM((batches * slots,), jnp.int32),
-            pltpu.VMEM((GROUP, 2, 2, window, LANES), f32),
-            pltpu.VMEM((2 * window, GROUP * window), bf16),
-            pltpu.VMEM((GROUP, window, 2 * window), bf16),
-            pltpu.VMEM((GROUP, 2 * window, 2 * window), bf16),
-        ],
+        scratch_shapes=scratch,
         compiler_params=pltpu.CompilerParams(vmem_limit_bytes=14 << 20),
-        name="slots",
-    )(
-        places, lives, obj, canvas, ya, yb, probe,
-        amplitudes.reshape(batches * slots, window, window), fwd, bwd, ext,
-    )
-    ya, yb = swap(ya, "row", 0), swap(yb, "row", 1)
+        name="outer",
+    )(places, lives, obj, canvas, ya, yb, probe, amps, fwd, bwd, ext)
+    ra, rb = swap(ra, "row", 0), swap(rb, "row", 1)
     scale = pl.pallas_call(
         light_kernel,
         out_shape=shape((tiles, tile_r, LANES), f32),
-        in_specs=[SMEM, VMEM],
+        in_specs=[VMEM] * 4,
         out_specs=VMEM,
         scratch_shapes=[
             pltpu.VMEM((2, window, LANES), f32),
             pltpu.VMEM((tiles + 4, tile_r + 2 * window, LANES), f32),
+            pltpu.VMEM((PACK, LANES), jnp.int32),
+            pltpu.SMEM((PACK, LANES), jnp.int32),
+            pltpu.SemaphoreType.DMA,
         ],
         compiler_params=pltpu.CompilerParams(vmem_limit_bytes=9 << 20),
         cost_estimate=pl.CostEstimate(flops=8 << 20, bytes_accessed=12 << 20, transcendentals=0),
         name="light",
-    )(table, probe)
+    )(meta, ya, yb, probe)
+    canvas, scale = lax.optimization_barrier((canvas, scale))
+    ya, yb = ra, rb
     rim = shape((2 * tile_r, LANES), bf16)
     sa, sb = pl.pallas_call(
         strips_kernel,

time: 84.5 us -> 67.1 us (0.79)
  the two profiles are of different devices: /device:TPU:34 before, /device:TPU:123 now
where the time goes in v1:
time: 67.1 us; the launch traced here: 66.4 us
  waiting for transfers between devices  24.7 us (37%)
  Pallas kernels  18 us (27%)
  starting transfers between devices  16.1 us (24%)
  other arithmetic  3.39 us (5%)
  local copies, waits for them, and re-layouts  3.33 us (5%)
  between operations  0.86 us (1%)
    ppermute x8, waiting for transfers between devices, swap(): return lax.ppermute(block, axis, route)  24.7 us
    ppermute x8, starting transfers between devices, swap(): return lax.ppermute(block, axis, route)  16.1 us
    pallas_call x1, Pallas kernels, on_device(): pl.pallas_call(light_kernel, out_shape=shape((tiles, tile_r, LANES), f32)...  4.44 us
    pallas_call x1, Pallas kernels, on_device(): pl.pallas_call(functools.partial(slots_kernel, True), out_shape=(shape(pa...  4.33 us
    pallas_call x1, Pallas kernels, on_device(): pl.pallas_call(update_kernel, grid=(tile_r // margin,), out_shape=(field,...  3.9 us
    pallas_call x1, Pallas kernels, on_device(): pl.pallas_call(edges_kernel, out_shape=(side, side), in_specs=[SMEM, SMEM...  3.03 us
    unnamed x15, local copies, waits for them, and re-layouts  2.7 us
  transfers between devices with their start and end apart: 8, of which 6 were waited for; matrix products, arithmetic and copies ran while one was open for 5% of the time, Pallas kernels for 10%

profile of v1, /device:TPU:123, one launch (start us, length us, event | category | flops | bytes accessed | tf_op | source)
XLA Modules:
  0.0 66.4 jit_solution(12613593997640884577)
XLA Ops:
  0.6 0.8 %copy.12 = s32[1,1,3,4,2]{4,3,2,1,0:T(4,128)S(1)} copy(s32[1,1,3,4,2]{3,4,2,1,0:T(2,128)} %param.8) | data formatting | bytes 192 | tf_op args[3]
  1.4 0.6 reshape.105.pos_ref.refs_0_
  2.0 3.0 %edges.1 = (bf16[1552,128]{1,0:T(8,128)(2,1)}, bf16[1552,128]{1,0:T(8,128)(2,1)}) custom-call(s32[24]{0:T(128)} %reshape.105.pos_ref.refs_0_, s32[3]{0:T(128)} %bitcast.6, f32[2,768,512]{2,1,0:T(8,128)} %obj_ref.1), custom_call_target="tpu_custom_call" | custom-call | tf_op jit(solution)/shard_map/edges/pallas_call | solution.py:418
  5.1 0.0 copy-start.4
  5.1 4.9 %collective-permute-start.1 = (bf16[1552,128]{1,0:T(8,128)(2,1)}, bf16[1552,128]{1,0:T(8,128)(2,1)S(1)}, u32[]{:S(2)}, u32[]{:S(2)}) collective-permute-start(bf16[1552,128]{1,0:T(8,128)(2,1)} %get-tuple-element.24), channel_id=1, source_target_pairs={{1,2},{2,1},{3,4},{4,3},{5,6},{6,5},{9,10},{10,9},{11,12},{12,11},... | collective-permute-start | bytes 1191944 | tf_op jit(solution)/shard_map/ppermute | solution.py:28
  10.0 0.1 collective-permute-start
  10.1 1.1 %multiply_convert_fusion.1 = (bf16[1,256,2,128]{3,1,2,0:T(8,128)(2,1)S(1)}, bf16[1,256,2,128]{3,1,2,0:T(8,128)(2,1)S(1)}) fusion(s32[2,128]{1,0:T(2,128)S(1)} %multiply_add_fusion), kind=kLoop, calls=%fused_computation.20 | loop fusion | flops 1245184 | bytes 263168 | tf_op jit(solution)/shard_map/convert_element_type | solution.py:41
  11.3 1.0 %fusion.14 = bf16[256,256]{1,0:T(8,128)(2,1)S(1)} fusion(), kind=kLoop, calls=%fused_computation.29 | loop fusion | flops 1310720 | bytes 131072 | tf_op jit(solution)/shard_map/neg | solution.py:408
  12.3 0.0 copy-start
  12.3 1.9 %copy-done = f32[2,768,512]{2,1,0:T(8,128)S(1)} copy-done((f32[2,768,512]{2,1,0:T(8,128)S(1)}, f32[2,768,512]{2,1,0:T(8,128)}, u32[]{:S(2)}) %copy-start) | copy-done | bytes 3145752
  14.2 1.1 %prepare.1 = (f32[2,6,1024,128]{3,2,1,0:T(8,128)S(1)}, f32[2,6,1024,128]{3,2,1,0:T(8,128)S(1)}) custom-call(f32[2,768,512]{2,1,0:T(8,128)S(1)} %copy-done), custom_call_target="tpu_custom_call" | custom-call | flops 4194304 | bytes 16777216 | tf_op jit(solution)/shard_map/prepare/pallas_call | solution.py:428
  15.3 1.1 %multiply_convert_fusion.2 = (bf16[256,256]{1,0:T(8,128)(2,1)S(1)}, bf16[256,256]{1,0:T(8,128)(2,1)S(1)}) fusion(), kind=kLoop, calls=%fused_computation.23 | loop fusion | flops 1245184 | bytes 262144 | tf_op jit(solution)/shard_map/convert_element_type | solution.py:42
  16.4 0.1 convert_bitcast_fusion.refs_8_.refs_10_
  16.5 0.1 fusion.1
  16.6 2.4 %collective-permute-done.1.zb_ref = bf16[1552,128]{1,0:T(8,128)(2,1)S(1)} collective-permute-done((bf16[1552,128]{1,0:T(8,128)(2,1)}, bf16[1552,128]{1,0:T(8,128)(2,1)S(1)}, u32[]{:S(2)}, u32[]{:S(2)}) %collective-permute-start.1) | collective-permute-done | bytes 397344 | tf_op jit(solution)/shard_map/ppermute | solution.py:28
  19.0 1.0 %collective-permute-done.za_ref = bf16[1552,128]{1,0:T(8,128)(2,1)S(1)} collective-permute-done((bf16[1552,128]{1,0:T(8,128)(2,1)}, bf16[1552,128]{1,0:T(8,128)(2,1)S(1)}, u32[]{:S(2)}, u32[]{:S(2)}) %collective-permute-start) | collective-permute-done | bytes 397344 | tf_op jit(solution)/shard_map/ppermute | solution.py:28
  20.1 0.2 sides.1
  20.3 2.0 %collective-permute-start.2 = (bf16[1584,128]{1,0:T(8,128)(2,1)S(1)}, bf16[1584,128]{1,0:T(8,128)(2,1)S(1)}, u32[]{:S(2)}, u32[]{:S(2)}) collective-permute-start(bf16[1584,128]{1,0:T(8,128)(2,1)S(1)} %get-tuple-element.30), channel_id=1, source_target_pairs={{0,8},{8,0},{16,24},{24,16},{32,40},{40,32},{48,56},{56,48},{64,72... | collective-permute-start | bytes 1216520 | tf_op jit(solution)/shard_map/ppermute | solution.py:28
  22.2 2.7 %collective-permute-start.3 = (bf16[1584,128]{1,0:T(8,128)(2,1)S(1)}, bf16[1584,128]{1,0:T(8,128)(2,1)S(1)}, u32[]{:S(2)}, u32[]{:S(2)}) collective-permute-start(bf16[1584,128]{1,0:T(8,128)(2,1)S(1)} %get-tuple-element.31), channel_id=1, source_target_pairs={{8,16},{16,8},{24,32},{32,24},{40,48},{48,40},{56,64},{64,56},{72,... | collective-permute-start | bytes 1216520 | tf_op jit(solution)/shard_map/ppermute | solution.py:28
  25.0 0.8 %inner.1.refs_3_ = f32[2,6,1024,128]{3,2,1,0:T(8,128)S(1)} custom-call(s32[24]{0:T(128)S(1)} %copy-done.5, s32[3]{0:T(128)S(1)} %bitcast.7, f32[2,6,1024,128]{3,2,1,0:T(8,128)S(1)} %get-tuple-element.25.refs_2_, f32[2,6,1024,128]{3,2,1,0:T(8,128)S(1)} %get-tuple-element.26.refs_3_, f32[2,256,256]{2,1,0:T(8,128)S(1)} %copy-done.3, ...), custom_call_target="tpu_custom_call", output_to_operand_aliasing={{}: (3, {})} | custom-call | flops 4294967296 | bytes 20971520 | tf_op jit(solution)/shard_map/inner/pallas_call | solution.py:458
  25.7 7.8 %collective-permute-done.3.refs_5_.yb_ref = bf16[1584,128]{1,0:T(8,128)(2,1)S(1)} collective-permute-done((bf16[1584,128]{1,0:T(8,128)(2,1)S(1)}, bf16[1584,128]{1,0:T(8,128)(2,1)S(1)}, u32[]{:S(2)}, u32[]{:S(2)}) %collective-permute-start.3) | collective-permute-done | bytes 405536 | tf_op jit(solution)/shard_map/ppermute | solution.py:28
  33.6 4.3 %outer.1 = (f32[2,6,1024,128]{3,2,1,0:T(8,128)S(1)}, f32[2,6,1024,128]{3,2,1,0:T(8,128)S(1)}, bf16[1536,128]{1,0:T(8,128)(2,1)S(1)}, bf16[1536,128]{1,0:T(8,128)(2,1)S(1)}) custom-call(s32[24]{0:T(128)S(1)} %copy-done.5, s32[3]{0:T(128)S(1)} %bitcast.8, ...), custom_call_target="tpu_custom_call", output_to_operand_aliasing={{0}: (2, {}), {1}: (3, {})} | custom-call | tf_op jit(solution)/shard_map/outer/pallas_call | solution.py:469
  37.9 0.1 collective-permute-start.4
  38.0 2.9 %collective-permute-start.5 = (bf16[1536,128]{1,0:T(8,128)(2,1)S(1)}, bf16[1536,128]{1,0:T(8,128)(2,1)S(1)}, u32[]{:S(2)}, u32[]{:S(2)}) collective-permute-start(bf16[1536,128]{1,0:T(8,128)(2,1)S(1)} %get-tuple-element.36), channel_id=1, source_target_pairs={{8,16},{16,8},{24,32},{32,24},{40,48},{48,40},{56,64},{64,56},{72,... | collective-permute-start | bytes 1179656 | tf_op jit(solution)/shard_map/ppermute | solution.py:28
  41.0 4.4 %light.1.scale_ref = f32[4,768,128]{2,1,0:T(8,128)S(1)} custom-call(bf16[48,128]{1,0:T(8,128)(2,1)S(1)} %get-tuple-element.33.meta_ref, bf16[1584,128]{1,0:T(8,128)(2,1)S(1)} %collective-permute-done.2.refs_4_.ya_ref, bf16[1584,128]{1,0:T(8,128)(2,1)S(1)} %collective-permute-done.3.refs_5_.yb_ref, f32[2,256,256]{2,1,0:T(8,128)S(1)} %copy-done.3), custom_call_target="tpu_custom_call" | custom-call | flops 8388608 | bytes 12582912 | tf_op jit(solution)/shard_map/light/pallas_call | solution.py:480
  45.4 4.1 %collective-permute-done.5.yb_ref = bf16[1536,128]{1,0:T(8,128)(2,1)S(1)} collective-permute-done((bf16[1536,128]{1,0:T(8,128)(2,1)S(1)}, bf16[1536,128]{1,0:T(8,128)(2,1)S(1)}, u32[]{:S(2)}, u32[]{:S(2)}) %collective-permute-start.5) | collective-permute-done | bytes 393248 | tf_op jit(solution)/shard_map/ppermute | solution.py:28
  49.5 0.2 strips.1
  49.6 0.1 collective-permute-start.6
  49.7 3.4 %collective-permute-start.7 = (bf16[1536,128]{1,0:T(8,128)(2,1)S(1)}, bf16[1536,128]{1,0:T(8,128)(2,1)S(1)}, u32[]{:S(2)}, u32[]{:S(2)}) collective-permute-start(bf16[1536,128]{1,0:T(8,128)(2,1)S(1)} %get-tuple-element.38), channel_id=1, source_target_pairs={{1,2},{2,1},{3,4},{4,3},{5,6},{6,5},{9,10},{10,9},{11,12},{12,11},... | collective-permute-start | bytes 1179656 | tf_op jit(solution)/shard_map/ppermute | solution.py:28
  53.1 6.3 %collective-permute-done.6.sa_ref = bf16[1536,128]{1,0:T(8,128)(2,1)S(1)} collective-permute-done((bf16[1536,128]{1,0:T(8,128)(2,1)S(1)}, bf16[1536,128]{1,0:T(8,128)(2,1)S(1)}, u32[]{:S(2)}, u32[]{:S(2)}) %collective-permute-start.6) | collective-permute-done | bytes 393248 | tf_op jit(solution)/shard_map/ppermute | solution.py:28
  59.4 3.1 %collective-permute-done.7.sb_ref = bf16[1536,128]{1,0:T(8,128)(2,1)S(1)} collective-permute-done((bf16[1536,128]{1,0:T(8,128)(2,1)S(1)}, bf16[1536,128]{1,0:T(8,128)(2,1)S(1)}, u32[]{:S(2)}, u32[]{:S(2)}) %collective-permute-start.7) | collective-permute-done | bytes 393248 | tf_op jit(solution)/shard_map/ppermute | solution.py:28
  62.5 3.9 %update.1 = (f32[2,768,512]{2,1,0:T(8,128)}, f32[2,768,512]{2,1,0:T(8,128)}) custom-call(f32[2,768,512]{2,1,0:T(8,128)S(1)} %copy-done.1, f32[2,6,1024,128]{3,2,1,0:T(8,128)S(1)} %get-tuple-element.34.canvas_ref, bf16[1536,128]{1,0:T(8,128)(2,1)S(1)} %collective-permute-done.4.ya_ref, bf16[1536,128]{1,0:T(8,128)(2,1)S(1)} %collective-permute-done.5.yb_ref, ...), custom_call_target="tpu_custom_call" | custom-call | tf_op jit(solution)/shard_map/update/pallas_call | solution.py:510
  (14 shorter events, 0.0 us)
Async XLA Ops:
  5.1 15.0 %copy-start.4 = (bf16[1552,128]{1,0:T(8,128)(2,1)S(1)}, bf16[1552,128]{1,0:T(8,128)(2,1)}, u32[]{:S(2)}) copy-start(bf16[1552,128]{1,0:T(8,128)(2,1)} %get-tuple-element.23.own_ref) | copy-start | bytes 1191940
  5.1 13.9 %collective-permute-start.1 = (bf16[1552,128]{1,0:T(8,128)(2,1)}, bf16[1552,128]{1,0:T(8,128)(2,1)S(1)}, u32[]{:S(2)}, u32[]{:S(2)}) collective-permute-start(bf16[1552,128]{1,0:T(8,128)(2,1)} %get-tuple-element.24), channel_id=1, source_target_pairs={{1,2},{2,1},{3,4},{4,3},{5,6},{6,5},{9,10},{10,9},{11,12},{12,11},... | collective-permute-start | bytes 1191944 | tf_op jit(solution)/shard_map/ppermute | solution.py:28
  10.0 10.0 %collective-permute-start = (bf16[1552,128]{1,0:T(8,128)(2,1)}, bf16[1552,128]{1,0:T(8,128)(2,1)S(1)}, u32[]{:S(2)}, u32[]{:S(2)}) collective-permute-start(bf16[1552,128]{1,0:T(8,128)(2,1)} %get-tuple-element.23.own_ref), channel_id=1, source_target_pairs={{0,1},{1,0},{2,3},{3,2},{4,5},{5,4},{6,7},{7,6},{8,9},{9,8},{10,11... | collective-permute-start | bytes 1191944 | tf_op jit(solution)/shard_map/ppermute | solution.py:28
  12.3 1.9 %copy-start = (f32[2,768,512]{2,1,0:T(8,128)S(1)}, f32[2,768,512]{2,1,0:T(8,128)}, u32[]{:S(2)}) copy-start(f32[2,768,512]{2,1,0:T(8,128)} %obj_ref.1) | copy-start | bytes 9437188
  14.1 10.8 %copy-start.2 = (bf16[1,1,3,4,256,256]{5,4,3,2,1,0:T(8,128)(2,1)S(1)}, bf16[1,1,3,4,256,256]{5,4,3,2,1,0:T(8,128)(2,1)}, u32[]{:S(2)}) copy-start(bf16[1,1,3,4,256,256]{5,4,3,2,1,0:T(8,128)(2,1)} %param.7) | copy-start | bytes 4718596
  14.1 10.8 %copy-start.3 = (f32[2,256,256]{2,1,0:T(8,128)S(1)}, f32[2,256,256]{2,1,0:T(8,128)}, u32[]{:S(2)}) copy-start(f32[2,256,256]{2,1,0:T(8,128)} %probe_ref.1) | copy-start | bytes 1572868
  14.2 10.8 %copy-start.5 = (s32[24]{0:T(128)S(1)}, s32[24]{0:T(128)}, u32[]{:S(2)}) copy-start(s32[24]{0:T(128)} %reshape.105.pos_ref.refs_0_) | copy-start | bytes 292
  14.2 10.8 %copy-start.6 = (s32[1,1,3]{2,1,0:T(1,128)S(1)}, s32[1,1,3]{2,1,0:T(1,128)}, u32[]{:S(2)}) copy-start(s32[1,1,3]{2,1,0:T(1,128)} %param.9) | copy-start | bytes 40
  20.3 5.4 %collective-permute-start.2 = (bf16[1584,128]{1,0:T(8,128)(2,1)S(1)}, bf16[1584,128]{1,0:T(8,128)(2,1)S(1)}, u32[]{:S(2)}, u32[]{:S(2)}) collective-permute-start(bf16[1584,128]{1,0:T(8,128)(2,1)S(1)} %get-tuple-element.30), channel_id=1, source_target_pairs={{0,8},{8,0},{16,24},{24,16},{32,40},{40,32},{48,56},{56,48},{64,72... | collective-permute-start | bytes 1216520 | tf_op jit(solution)/shard_map/ppermute | solution.py:28
  22.2 11.3 %collective-permute-start.3 = (bf16[1584,128]{1,0:T(8,128)(2,1)S(1)}, bf16[1584,128]{1,0:T(8,128)(2,1)S(1)}, u32[]{:S(2)}, u32[]{:S(2)}) collective-permute-start(bf16[1584,128]{1,0:T(8,128)(2,1)S(1)} %get-tuple-element.31), channel_id=1, source_target_pairs={{8,16},{16,8},{24,32},{32,24},{40,48},{48,40},{56,64},{64,56},{72,... | collective-permute-start | bytes 1216520 | tf_op jit(solution)/shard_map/ppermute | solution.py:28
  37.9 24.6 %copy-start.1 = (f32[2,768,512]{2,1,0:T(8,128)S(1)}, f32[2,768,512]{2,1,0:T(8,128)}, u32[]{:S(2)}) copy-start(f32[2,768,512]{2,1,0:T(8,128)} %obj_ref.1) | copy-start | bytes 9437188
  37.9 7.5 %collective-permute-start.4 = (bf16[1536,128]{1,0:T(8,128)(2,1)S(1)}, bf16[1536,128]{1,0:T(8,128)(2,1)S(1)}, u32[]{:S(2)}, u32[]{:S(2)}) collective-permute-start(bf16[1536,128]{1,0:T(8,128)(2,1)S(1)} %get-tuple-element.35), channel_id=1, source_target_pairs={{0,8},{8,0},{16,24},{24,16},{32,40},{40,32},{48,56},{56,48},{64,72... | collective-permute-start | bytes 1179656 | tf_op jit(solution)/shard_map/ppermute | solution.py:28
  38.0 11.5 %collective-permute-start.5 = (bf16[1536,128]{1,0:T(8,128)(2,1)S(1)}, bf16[1536,128]{1,0:T(8,128)(2,1)S(1)}, u32[]{:S(2)}, u32[]{:S(2)}) collective-permute-start(bf16[1536,128]{1,0:T(8,128)(2,1)S(1)} %get-tuple-element.36), channel_id=1, source_target_pairs={{8,16},{16,8},{24,32},{32,24},{40,48},{48,40},{56,64},{64,56},{72,... | collective-permute-start | bytes 1179656 | tf_op jit(solution)/shard_map/ppermute | solution.py:28
  49.6 9.8 %collective-permute-start.6 = (bf16[1536,128]{1,0:T(8,128)(2,1)S(1)}, bf16[1536,128]{1,0:T(8,128)(2,1)S(1)}, u32[]{:S(2)}, u32[]{:S(2)}) collective-permute-start(bf16[1536,128]{1,0:T(8,128)(2,1)S(1)} %get-tuple-element.37), channel_id=1, source_target_pairs={{0,1},{1,0},{2,3},{3,2},{4,5},{5,4},{6,7},{7,6},{8,9},{9,8},{10,11... | collective-permute-start | bytes 1179656 | tf_op jit(solution)/shard_map/ppermute | solution.py:28
  49.7 12.8 %collective-permute-start.7 = (bf16[1536,128]{1,0:T(8,128)(2,1)S(1)}, bf16[1536,128]{1,0:T(8,128)(2,1)S(1)}, u32[]{:S(2)}, u32[]{:S(2)}) collective-permute-start(bf16[1536,128]{1,0:T(8,128)(2,1)S(1)} %get-tuple-element.38), channel_id=1, source_target_pairs={{1,2},{2,1},{3,4},{4,3},{5,6},{6,5},{9,10},{10,9},{11,12},{12,11},... | collective-permute-start | bytes 1179656 | tf_op jit(solution)/shard_map/ppermute | solution.py:28

commit v2 on v1

--- a/solution.py
+++ b/solution.py
@@ -44,41 +44,41 @@
 
 
 def meta_rows(pos_ref, counts_ref):
-    slots = pos_ref.shape[0] // 2
+    batches, slots = pos_ref.shape[2], pos_ref.shape[4]
     lane = lax.broadcasted_iota(jnp.int32, (PACK, LANES), 1)
     row = jnp.zeros((PACK, LANES), jnp.int32)
-    for k in range(2 * slots):
-        value = pos_ref[k] + LANES
+    fields = 2 * batches * slots
+    for k in range(fields):
+        value = pos_ref[0, 0, k // (2 * slots), k % 2, k // 2 % slots] + LANES
         row = jnp.where(lane == k, value // 16, row)
-        row = jnp.where(lane == 2 * slots + k, lax.rem(value, 16), row)
-    for k in range(counts_ref.shape[0]):
-        row = jnp.where(lane == 4 * slots + k, counts_ref[k], row)
+        row = jnp.where(lane == fields + k, lax.rem(value, 16), row)
+    for k in range(batches):
+        row = jnp.where(lane == 2 * fields + k, counts_ref[0, 0, k], row)
     return row.astype(f32).astype(bf16)
 
 
 def edges_kernel(pos_ref, counts_ref, obj_hbm, first_ref, second_ref, low, high, sem):
     tile_r, tile_c = obj_hbm.shape[1:]
+    part = 256
     copies = []
-    for c in range(2):
-        copies.append(pltpu.make_async_copy(obj_hbm.at[c, :, pl.ds(0, LANES)], low.at[c], sem.at[0, c]))
-        copies.append(
-            pltpu.make_async_copy(obj_hbm.at[c, :, pl.ds(tile_c - LANES, LANES)], high.at[c], sem.at[1, c])
-        )
+    for k in range(2 * tile_r // part):
+        c, r = divmod(k * part, tile_r)
+        for side, (start, target) in enumerate(((0, low), (tile_c - LANES, high))):
+            source = obj_hbm.at[c, pl.ds(r, part), pl.ds(start, LANES)]
+            copies.append(pltpu.make_async_copy(source, target.at[pl.ds(k * part, part), :], sem.at[side, k]))
     for copy in copies:
         copy.start()
     upward = even("col")
     meta = meta_rows(pos_ref, counts_ref)
     first_ref[2 * tile_r :, :] = meta
     second_ref[2 * tile_r :, :] = meta
-    for copy in copies:
-        copy.wait()
-    for c in range(2):
-        for r in range(0, tile_r, 128):
-            a = low[c, r : r + 128, :]
-            b = high[c, r : r + 128, :]
-            rows = slice(c * tile_r + r, c * tile_r + r + 128)
-            first_ref[rows, :] = jnp.where(upward, b, a).astype(bf16)
-            second_ref[rows, :] = jnp.where(upward, a, b).astype(bf16)
+    for k in range(2 * tile_r // part):
+        copies[2 * k].wait()
+        copies[2 * k + 1].wait()
+        rows = slice(k * part, (k + 1) * part)
+        a, b = low[rows, :], high[rows, :]
+        first_ref[rows, :] = jnp.where(upward, b, a).astype(bf16)
+        second_ref[rows, :] = jnp.where(upward, a, b).astype(bf16)
 
 
 def prepare_kernel(obj_hbm, obj_ref, canvas_ref, sem):
@@ -141,8 +141,7 @@
     else:
         (pos_ref, counts_ref, obj, canvas_in, probe_ref, amp_ref, fwd_ref, bwd_ref, ext_ref,
          canvas_ref, todo, prb, xs, hs, er) = refs
-    batches = counts_ref.shape[0]
-    slots = pos_ref.shape[0] // (2 * batches)
+    batches, slots = pos_ref.shape[2], pos_ref.shape[4]
     win = probe_ref.shape[1]
     margin = win // 2
     tiles = obj.shape[1] - 2
@@ -158,9 +157,9 @@
 
     def collect(slot, count):
         batch = slot // slots
-        row = pos_ref[2 * slot]
+        row = pos_ref[0, 0, batch, 0, slot - batch * slots]
         inside = (row >= 0) & (row <= tile_r - win)
-        live = (slot - batch * slots < counts_ref[batch]) & (inside != outer)
+        live = (slot - batch * slots < counts_ref[0, 0, batch]) & (inside != outer)
 
         @pl.when(live)
         def _():
@@ -176,8 +175,9 @@
         for g in range(GROUP):
             at = p * GROUP + g
             slot = todo[jnp.minimum(at, total - 1)]
-            row = pos_ref[2 * slot] + margin
-            col = pos_ref[2 * slot + 1] + margin
+            batch = slot // slots
+            row = pos_ref[0, 0, batch, 0, slot - batch * slots] + margin
+            col = pos_ref[0, 0, batch, 1, slot - batch * slots] + margin
             tile = col // LANES
             shift = col - tile * LANES
             chosen.append((slot, row, tile, jnp.minimum(tile + 2, tiles + 1), shift, at < total))
@@ -359,42 +359,50 @@
             sb_ref[rows, :] = jnp.where(right_first, sides[0], sides[1]).astype(bf16)
 
 
-def update_kernel(obj_ref, canvas_ref, ya_ref, yb_ref, sa_ref, sb_ref, scale_ref, grad_ref, out_ref):
+def update_kernel(outer, *refs):
+    if outer:
+        obj_ref, canvas_ref, ya_ref, yb_ref, scale_ref, sa_ref, sb_ref, _, _, grad_hbm, out_hbm, grad, out, sem = refs
+    else:
+        obj_ref, canvas_ref, ya_ref, yb_ref, scale_ref, grad_hbm, out_hbm, grad, out, sem = refs
     tiles = canvas_ref.shape[1] - 2
     margin = LANES
     tile_r = canvas_ref.shape[2] - 2 * margin
-    step = pl.program_id(0)
+    part = 256
     lower_first = even("row")
     right_first = even("col")
-    first = step == 0
-    last = step == pl.num_programs(0) - 1
-    start = pl.multiple_of(step * margin, margin)
-    def write(edge):
-        for c in range(2):
-            for t in range(tiles):
-                value = canvas_ref[c, t + 1, pl.ds(margin + start, margin), :]
-                if edge:
-                    k = (c * (tiles + 2) + t + 1) * margin
-                    a, b = ya_ref[k : k + margin, :].astype(f32), yb_ref[k : k + margin, :].astype(f32)
-                    value += jnp.where(lower_first == first, b, a)
-                if t in (0, tiles - 1):
-                    rows = pl.ds(pl.multiple_of(c * tile_r + start, margin), margin)
-                    a, b = sa_ref[rows, :].astype(f32), sb_ref[rows, :].astype(f32)
-                    if t == 0:
-                        value += jnp.where(right_first, b, a)
-                    if t == tiles - 1:
-                        value += jnp.where(right_first, a, b)
-                cols = slice(LANES * t, LANES * (t + 1))
-                grad_ref[c, :, cols] = value
-                out_ref[c, :, cols] = obj_ref[c, :, cols] - scale_ref[t, pl.ds(start, margin), :] * value
-
-    @pl.when(first | last)
-    def _():
-        write(True)
-
-    @pl.when(jnp.logical_not(first | last))
-    def _():
-        write(False)
+    copies = []
+    for r in range(0, tile_r, part):
+        for k, t in enumerate((0, tiles - 1) if outer else range(1, tiles - 1)):
+            cols = slice(LANES * t, LANES * (t + 1))
+            rows = slice(r, r + part)
+            for c in range(2):
+                value = canvas_ref[c, t + 1, margin + r : margin + r + part, :]
+                if outer:
+                    at = slice(c * tile_r + r, c * tile_r + r + part)
+                    a, b = sa_ref[at, :].astype(f32), sb_ref[at, :].astype(f32)
+                    value += jnp.where(right_first, b, a) if t == 0 else jnp.where(right_first, a, b)
+                at = (c * (tiles + 2) + t + 1) * margin
+                if r == 0 or r + part == tile_r:
+                    a = ya_ref[at : at + margin, :].astype(f32)
+                    b = yb_ref[at : at + margin, :].astype(f32)
+                    if r == 0:
+                        top = value[:margin] + jnp.where(lower_first, b, a)
+                        value = jnp.concatenate([top, value[margin:]], 0)
+                    else:
+                        bottom = value[part - margin :] + jnp.where(lower_first, a, b)
+                        value = jnp.concatenate([value[: part - margin], bottom], 0)
+                grad[c, k, rows, :] = value
+                out[c, k, rows, :] = obj_ref[c, rows, cols] - scale_ref[t, rows, :] * value
+            for n, (source, target) in enumerate(((grad, grad_hbm), (out, out_hbm))):
+                copy = pltpu.make_async_copy(
+                    source.at[:, k, pl.ds(r, part), :],
+                    target.at[:, pl.ds(r, part), pl.ds(LANES * t, LANES)],
+                    sem.at[n, k, r // part],
+                )
+                copy.start()
+                copies.append(copy)
+    for copy in copies:
+        copy.wait()
 
 
 def on_device(object_field, probe, amplitudes, positions, counts):
@@ -409,8 +417,7 @@
     bwd = jnp.concatenate([jnp.concatenate([real, imag], 1), jnp.concatenate([-imag, real], 1)], 0)
     tables = jnp.stack([real, imag]).astype(f32)
     ext = jnp.concatenate([tables, tables], 1).reshape(2, 2 * window, 2, LANES).transpose(0, 2, 1, 3)
-    places = positions.reshape(2 * batches * slots)
-    lives = counts.reshape(batches)
+    places = jnp.swapaxes(positions, 3, 4)
     shape = jax.ShapeDtypeStruct
     side = shape((2 * tile_r + PACK, LANES), bf16)
     strip = shape((2 * (tiles + 2) * margin, LANES), bf16)
@@ -420,9 +427,9 @@
         out_shape=(side, side),
         in_specs=[SMEM, SMEM, ANY],
         out_specs=(VMEM, VMEM),
-        scratch_shapes=[pltpu.VMEM((2, tile_r, LANES), f32)] * 2 + [pltpu.SemaphoreType.DMA((2, 2))],
+        scratch_shapes=[pltpu.VMEM((2 * tile_r, LANES), f32)] * 2 + [pltpu.SemaphoreType.DMA((2, 2 * tile_r // 256))],
         name="edges",
-    )(places, lives, object_field)
+    )(places, counts, object_field)
     own = za
     za, zb = swap(za, "col", 0), swap(zb, "col", 1)
     obj, canvas = pl.pallas_call(
@@ -465,7 +472,7 @@
         compiler_params=pltpu.CompilerParams(vmem_limit_bytes=14 << 20),
         cost_estimate=pl.CostEstimate(flops=4 << 30, bytes_accessed=20 << 20, transcendentals=0),
         name="inner",
-    )(places, lives, obj, canvas, probe, amps, fwd, bwd, ext)
+    )(places, counts, obj, canvas, probe, amps, fwd, bwd, ext)
     _, canvas, ra, rb = pl.pallas_call(
         functools.partial(slots_kernel, True),
         out_shape=(shape(padded, f32), shape(padded, f32), strip, strip),
@@ -475,7 +482,7 @@
         scratch_shapes=scratch,
         compiler_params=pltpu.CompilerParams(vmem_limit_bytes=14 << 20),
         name="outer",
-    )(places, lives, obj, canvas, ya, yb, probe, amps, fwd, bwd, ext)
+    )(places, counts, obj, canvas, ya, yb, probe, amps, fwd, bwd, ext)
     ra, rb = swap(ra, "row", 0), swap(rb, "row", 1)
     scale = pl.pallas_call(
         light_kernel,
@@ -494,7 +501,6 @@
         name="light",
     )(meta, ya, yb, probe)
     canvas, scale = lax.optimization_barrier((canvas, scale))
-    ya, yb = ra, rb
     rim = shape((2 * tile_r, LANES), bf16)
     sa, sb = pl.pallas_call(
         strips_kernel,
@@ -503,19 +509,26 @@
         out_specs=(VMEM, VMEM),
         compiler_params=pltpu.CompilerParams(vmem_limit_bytes=4 << 20),
         name="strips",
-    )(canvas, ya, yb)
+    )(canvas, ra, rb)
     sa, sb = swap(sa, "col", 0), swap(sb, "col", 1)
-    block = pl.BlockSpec((2, margin, tile_c), lambda i: (0, i, 0))
     field = shape((2, tile_r, tile_c), f32)
-    return pl.pallas_call(
-        update_kernel,
-        grid=(tile_r // margin,),
-        out_shape=(field, field),
-        in_specs=[block] + [VMEM] * 6,
-        out_specs=(block, block),
-        compiler_params=pltpu.CompilerParams(vmem_limit_bytes=8 << 20),
-        name="update",
-    )(object_field, canvas, ya, yb, sa, sb, scale)
+
+    def update(outer, aliases, *args):
+        return pl.pallas_call(
+            functools.partial(update_kernel, outer),
+            out_shape=(field, field),
+            in_specs=[VMEM] * (7 if outer else 5) + [ANY] * len(aliases),
+            out_specs=(ANY, ANY),
+            input_output_aliases=aliases,
+            scratch_shapes=[pltpu.VMEM((2, 2, tile_r, LANES), f32)] * 2
+            + [pltpu.SemaphoreType.DMA((2, 2, tile_r // 256))],
+            compiler_params=pltpu.CompilerParams(vmem_limit_bytes=8 << 20),
+            cost_estimate=pl.CostEstimate(flops=4 << 20, bytes_accessed=10 << 20, transcendentals=0),
+            name="rims" if outer else "middle",
+        )(*args)
+
+    grad, out = update(False, {}, object_field, canvas, ra, rb, scale)
+    return update(True, {7: 0, 8: 1}, object_field, canvas, ra, rb, scale, sa, sb, grad, out)
 
 
 def solution(mesh):

time: 67.1 us -> 64.5 us (0.961)
  local copies, waits for them, and re-layouts: 3.33 us -> 0.04 us
  starting transfers between devices: 16.1 us -> 17 us
  waiting for transfers between devices: 24.7 us -> 23.8 us
    unnamed x15 -> x12, local copies, waits for them, and re-layouts: 2.7 us -> 0.04 us
    pallas_call x1, Pallas kernels: 0.76 us -> 2.54 us  [on_device(): pl.pallas_call(functools.partial(slots_kernel, False), out_shape=shape(pa...]
    pallas_call x1, Pallas kernels: 4.33 us -> 2.72 us  [on_device(): pl.pallas_call(functools.partial(slots_kernel, True), out_shape=(shape(pa...]
    ppermute x8, starting transfers between devices: 16.1 us -> 17 us  [swap(): return lax.ppermute(block, axis, route)]
    ppermute x8, waiting for transfers between devices: 24.7 us -> 23.8 us  [swap(): return lax.ppermute(block, axis, route)]
    pallas_call x1 -> x2, Pallas kernels: 3.9 us -> 3.67 us  [update(): pl.pallas_call(functools.partial(update_kernel, outer), out_shape=(field,...]
  transfers between devices with their start and end apart: 8 -> 8, of which waited for: 6 -> 6; matrix products, arithmetic and copies ran while one was open for 5% -> 5% of each run, Pallas kernels for 10% -> 15%
where the time goes in v2:
time: 64.5 us; the launch traced here: 63.3 us
  waiting for transfers between devices  23.8 us (37%)
  Pallas kernels  18.1 us (28%)
  starting transfers between devices  17 us (26%)
  other arithmetic  3.39 us (5%)
  between operations  0.87 us (1%)
    ppermute x8, waiting for transfers between devices, swap(): return lax.ppermute(block, axis, route)  23.8 us
    ppermute x8, starting transfers between devices, swap(): return lax.ppermute(block, axis, route)  17 us
    pallas_call x1, Pallas kernels, on_device(): pl.pallas_call(light_kernel, out_shape=shape((tiles, tile_r, LANES), f32)...  4.28 us
    pallas_call x2, Pallas kernels, update(): pl.pallas_call(functools.partial(update_kernel, outer), out_shape=(field,...  3.67 us
    pallas_call x1, Pallas kernels, on_device(): pl.pallas_call(edges_kernel, out_shape=(side, side), in_specs=[SMEM, SMEM...  3.39 us
    pallas_call x1, Pallas kernels, on_device(): pl.pallas_call(functools.partial(slots_kernel, True), out_shape=(shape(pa...  2.72 us
    pallas_call x1, Pallas kernels, on_device(): pl.pallas_call(functools.partial(slots_kernel, False), out_shape=shape(pa...  2.54 us
  transfers between devices with their start and end apart: 8, of which 6 were waited for; matrix products, arithmetic and copies ran while one was open for 5% of the time, Pallas kernels for 15%

profile of v2, /device:TPU:123, one launch (start us, length us, event | category | flops | bytes accessed | tf_op | source)
XLA Modules:
  0.0 63.3 jit_solution(16475784756653005415)
XLA Ops:
  0.6 3.4 %edges.1 = (bf16[1552,128]{1,0:T(8,128)(2,1)}, bf16[1552,128]{1,0:T(8,128)(2,1)}) custom-call(s32[1,1,3,2,4]{4,3,2,1,0:T(2,128)} %bitcast.6, s32[1,1,3]{2,1,0:T(1,128)} %refs_1_.3, f32[2,768,512]{2,1,0:T(8,128)} %refs_0_.3), custom_call_target="tpu_custom_call" | custom-call | tf_op jit(solution)/shard_map/edges/pallas_call | solution.py:425
  4.0 4.8 %collective-permute-start.1 = (bf16[1552,128]{1,0:T(8,128)(2,1)}, bf16[1552,128]{1,0:T(8,128)(2,1)S(1)}, u32[]{:S(2)}, u32[]{:S(2)}) collective-permute-start(bf16[1552,128]{1,0:T(8,128)(2,1)} %get-tuple-element.26), channel_id=1, source_target_pairs={{1,2},{2,1},{3,4},{4,3},{5,6},{6,5},{9,10},{10,9},{11,12},{12,11},... | collective-permute-start | bytes 1191944 | tf_op jit(solution)/shard_map/ppermute | solution.py:28
  8.8 0.1 collective-permute-start
  8.9 1.1 %multiply_convert_fusion.1 = (bf16[1,256,2,128]{3,1,2,0:T(8,128)(2,1)S(1)}, bf16[1,256,2,128]{3,1,2,0:T(8,128)(2,1)S(1)}) fusion(s32[2,128]{1,0:T(2,128)S(1)} %multiply_add_fusion), kind=kLoop, calls=%fused_computation.20 | loop fusion | flops 1245184 | bytes 263168 | tf_op jit(solution)/shard_map/convert_element_type | solution.py:41
  10.1 0.0 copy-start.3
  10.1 1.0 %fusion.14 = bf16[256,256]{1,0:T(8,128)(2,1)S(1)} fusion(), kind=kLoop, calls=%fused_computation.29 | loop fusion | flops 1310720 | bytes 131072 | tf_op jit(solution)/shard_map/neg | solution.py:416
  11.1 1.1 %prepare.1 = (f32[2,6,1024,128]{3,2,1,0:T(8,128)S(1)}, f32[2,6,1024,128]{3,2,1,0:T(8,128)S(1)}) custom-call(f32[2,768,512]{2,1,0:T(8,128)S(1)} %copy-done), custom_call_target="tpu_custom_call" | custom-call | flops 4194304 | bytes 16777216 | tf_op jit(solution)/shard_map/prepare/pallas_call | solution.py:435
  12.2 1.1 %multiply_convert_fusion.2 = (bf16[256,256]{1,0:T(8,128)(2,1)S(1)}, bf16[256,256]{1,0:T(8,128)(2,1)S(1)}) fusion(), kind=kLoop, calls=%fused_computation.23 | loop fusion | flops 1245184 | bytes 262144 | tf_op jit(solution)/shard_map/convert_element_type | solution.py:42
  13.3 0.1 convert_bitcast_fusion.refs_8_.refs_10_
  13.4 0.1 fusion.1
  13.5 0.0 copy-start.1
  13.5 0.0 copy-start.2
  13.5 0.0 copy-start.4
  13.5 4.3 %collective-permute-done.1.zb_ref = bf16[1552,128]{1,0:T(8,128)(2,1)S(1)} collective-permute-done((bf16[1552,128]{1,0:T(8,128)(2,1)}, bf16[1552,128]{1,0:T(8,128)(2,1)S(1)}, u32[]{:S(2)}, u32[]{:S(2)}) %collective-permute-start.1) | collective-permute-done | bytes 397344 | tf_op jit(solution)/shard_map/ppermute | solution.py:28
  17.8 1.0 %collective-permute-done.za_ref = bf16[1552,128]{1,0:T(8,128)(2,1)S(1)} collective-permute-done((bf16[1552,128]{1,0:T(8,128)(2,1)}, bf16[1552,128]{1,0:T(8,128)(2,1)S(1)}, u32[]{:S(2)}, u32[]{:S(2)}) %collective-permute-start) | collective-permute-done | bytes 397344 | tf_op jit(solution)/shard_map/ppermute | solution.py:28
  18.8 0.2 sides.1
  19.1 2.0 %collective-permute-start.2 = (bf16[1584,128]{1,0:T(8,128)(2,1)S(1)}, bf16[1584,128]{1,0:T(8,128)(2,1)S(1)}, u32[]{:S(2)}, u32[]{:S(2)}) collective-permute-start(bf16[1584,128]{1,0:T(8,128)(2,1)S(1)} %get-tuple-element.32), channel_id=1, source_target_pairs={{0,8},{8,0},{16,24},{24,16},{32,40},{40,32},{48,56},{56,48},{64,72... | collective-permute-start | bytes 1216520 | tf_op jit(solution)/shard_map/ppermute | solution.py:28
  21.0 2.7 %collective-permute-start.3 = (bf16[1584,128]{1,0:T(8,128)(2,1)S(1)}, bf16[1584,128]{1,0:T(8,128)(2,1)S(1)}, u32[]{:S(2)}, u32[]{:S(2)}) collective-permute-start(bf16[1584,128]{1,0:T(8,128)(2,1)S(1)} %get-tuple-element.33), channel_id=1, source_target_pairs={{8,16},{16,8},{24,32},{32,24},{40,48},{48,40},{56,64},{64,56},{72,... | collective-permute-start | bytes 1216520 | tf_op jit(solution)/shard_map/ppermute | solution.py:28
  23.7 2.5 %inner.1.refs_3_ = f32[2,6,1024,128]{3,2,1,0:T(8,128)S(1)} custom-call(s32[1,1,3,2,4]{4,3,2,1,0:T(2,128)S(1)} %bitcast.7, s32[1,1,3]{2,1,0:T(1,128)S(1)} %copy-done.5, f32[2,6,1024,128]{3,2,1,0:T(8,128)S(1)} %get-tuple-element.27.refs_2_, f32[2,6,1024,128]{3,2,1,0:T(8,128)S(1)} %get-tuple-element.28.refs_3_, ...), custom_call_target="tpu_custom_call", output_to_operand_aliasing={{}: (3, {})} | custom-call | flops 4294967296 | bytes 20971520 | tf_op jit(solution)/shard_map/inner/pallas_call | solution.py:465
  26.3 6.0 %collective-permute-done.3.refs_5_.yb_ref = bf16[1584,128]{1,0:T(8,128)(2,1)S(1)} collective-permute-done((bf16[1584,128]{1,0:T(8,128)(2,1)S(1)}, bf16[1584,128]{1,0:T(8,128)(2,1)S(1)}, u32[]{:S(2)}, u32[]{:S(2)}) %collective-permute-start.3) | collective-permute-done | bytes 405536 | tf_op jit(solution)/shard_map/ppermute | solution.py:28
  32.3 2.7 %outer.1 = (f32[2,6,1024,128]{3,2,1,0:T(8,128)S(1)}, f32[2,6,1024,128]{3,2,1,0:T(8,128)S(1)}, bf16[1536,128]{1,0:T(8,128)(2,1)S(1)}, bf16[1536,128]{1,0:T(8,128)(2,1)S(1)}) custom-call(s32[1,1,3,2,4]{4,3,2,1,0:T(2,128)S(1)} %bitcast.8, s32[1,1,3]{2,1,0:T(1,128)S(1)} %copy-done.5, ...), custom_call_target="tpu_custom_call", output_to_operand_aliasing={{0}: (2, {}), {1}: (3, {})} | custom-call | tf_op jit(solution)/shard_map/outer/pallas_call | solution.py:476
  35.1 0.1 collective-permute-start.4
  35.2 2.7 %collective-permute-start.5 = (bf16[1536,128]{1,0:T(8,128)(2,1)S(1)}, bf16[1536,128]{1,0:T(8,128)(2,1)S(1)}, u32[]{:S(2)}, u32[]{:S(2)}) collective-permute-start(bf16[1536,128]{1,0:T(8,128)(2,1)S(1)} %get-tuple-element.38), channel_id=1, source_target_pairs={{8,16},{16,8},{24,32},{32,24},{40,48},{48,40},{56,64},{64,56},{72,... | collective-permute-start | bytes 1179656 | tf_op jit(solution)/shard_map/ppermute | solution.py:28
  37.9 4.3 %light.1.refs_4_ = f32[4,768,128]{2,1,0:T(8,128)S(1)} custom-call(bf16[48,128]{1,0:T(8,128)(2,1)S(1)} %get-tuple-element.35.meta_ref, bf16[1584,128]{1,0:T(8,128)(2,1)S(1)} %collective-permute-done.2.refs_4_.ya_ref, bf16[1584,128]{1,0:T(8,128)(2,1)S(1)} %collective-permute-done.3.refs_5_.yb_ref, f32[2,256,256]{2,1,0:T(8,128)S(1)} %copy-done.2), custom_call_target="tpu_custom_call" | custom-call | flops 8388608 | bytes 12582912 | tf_op jit(solution)/shard_map/light/pallas_call | solution.py:487
  42.2 4.2 %collective-permute-done.5.yb_ref.refs_3_ = bf16[1536,128]{1,0:T(8,128)(2,1)S(1)} collective-permute-done((bf16[1536,128]{1,0:T(8,128)(2,1)S(1)}, bf16[1536,128]{1,0:T(8,128)(2,1)S(1)}, u32[]{:S(2)}, u32[]{:S(2)}) %collective-permute-start.5) | collective-permute-done | bytes 393248 | tf_op jit(solution)/shard_map/ppermute | solution.py:28
  46.4 0.2 strips.1
  46.6 1.8 %collective-permute-start.6 = (bf16[1536,128]{1,0:T(8,128)(2,1)S(1)}, bf16[1536,128]{1,0:T(8,128)(2,1)S(1)}, u32[]{:S(2)}, u32[]{:S(2)}) collective-permute-start(bf16[1536,128]{1,0:T(8,128)(2,1)S(1)} %get-tuple-element.40), channel_id=1, source_target_pairs={{0,1},{1,0},{2,3},{3,2},{4,5},{5,4},{6,7},{7,6},{8,9},{9,8},{10,11... | collective-permute-start | bytes 1179656 | tf_op jit(solution)/shard_map/ppermute | solution.py:28
  48.4 2.9 %collective-permute-start.7 = (bf16[1536,128]{1,0:T(8,128)(2,1)S(1)}, bf16[1536,128]{1,0:T(8,128)(2,1)S(1)}, u32[]{:S(2)}, u32[]{:S(2)}) collective-permute-start(bf16[1536,128]{1,0:T(8,128)(2,1)S(1)} %get-tuple-element.41), channel_id=1, source_target_pairs={{1,2},{2,1},{3,4},{4,3},{5,6},{6,5},{9,10},{10,9},{11,12},{12,11},... | collective-permute-start | bytes 1179656 | tf_op jit(solution)/shard_map/ppermute | solution.py:28
  51.3 1.8 %middle.1 = (f32[2,768,512]{2,1,0:T(8,128)}, f32[2,768,512]{2,1,0:T(8,128)}) custom-call(f32[2,768,512]{2,1,0:T(8,128)S(1)} %copy-done, f32[2,6,1024,128]{3,2,1,0:T(8,128)S(1)} %get-tuple-element.36.canvas_ref.refs_1_, bf16[1536,128]{1,0:T(8,128)(2,1)S(1)} %collective-permute-done.4.ya_ref.refs_2_, ...), custom_call_target="tpu_custom_call" | custom-call | flops 4194304 | bytes 10485760 | tf_op jit(solution)/shard_map/middle/pallas_call | solution.py:517
  53.1 3.5 %collective-permute-done.6.refs_5_ = bf16[1536,128]{1,0:T(8,128)(2,1)S(1)} collective-permute-done((bf16[1536,128]{1,0:T(8,128)(2,1)S(1)}, bf16[1536,128]{1,0:T(8,128)(2,1)S(1)}, u32[]{:S(2)}, u32[]{:S(2)}) %collective-permute-start.6) | collective-permute-done | bytes 393248 | tf_op jit(solution)/shard_map/ppermute | solution.py:28
  56.6 4.8 %collective-permute-done.7.refs_6_ = bf16[1536,128]{1,0:T(8,128)(2,1)S(1)} collective-permute-done((bf16[1536,128]{1,0:T(8,128)(2,1)S(1)}, bf16[1536,128]{1,0:T(8,128)(2,1)S(1)}, u32[]{:S(2)}, u32[]{:S(2)}) %collective-permute-start.7) | collective-permute-done | bytes 393248 | tf_op jit(solution)/shard_map/ppermute | solution.py:28
  61.4 1.9 %rims.1 = (f32[2,768,512]{2,1,0:T(8,128)}, f32[2,768,512]{2,1,0:T(8,128)}) custom-call(f32[2,768,512]{2,1,0:T(8,128)S(1)} %copy-done, f32[2,6,1024,128]{3,2,1,0:T(8,128)S(1)} %get-tuple-element.36.canvas_ref.refs_1_, bf16[1536,128]{1,0:T(8,128)(2,1)S(1)} %collective-permute-done.4.ya_ref.refs_2_, ...), custom_call_target="tpu_custom_call", output_to_operand_aliasing={{0}: (7, {}), {1}: (8, {})} | custom-call | flops 4194304 | bytes 10485760 | tf_op jit(solution)/shard_map/rims/pallas_call | solution.py:517
  (11 shorter events, 0.0 us)
Async XLA Ops:
  0.6 10.4 %copy-start = (f32[2,768,512]{2,1,0:T(8,128)S(1)}, f32[2,768,512]{2,1,0:T(8,128)}, u32[]{:S(2)}) copy-start(f32[2,768,512]{2,1,0:T(8,128)} %refs_0_.3) | copy-start | bytes 9437188
  4.0 13.8 %collective-permute-start.1 = (bf16[1552,128]{1,0:T(8,128)(2,1)}, bf16[1552,128]{1,0:T(8,128)(2,1)S(1)}, u32[]{:S(2)}, u32[]{:S(2)}) collective-permute-start(bf16[1552,128]{1,0:T(8,128)(2,1)} %get-tuple-element.26), channel_id=1, source_target_pairs={{1,2},{2,1},{3,4},{4,3},{5,6},{6,5},{9,10},{10,9},{11,12},{12,11},... | collective-permute-start | bytes 1191944 | tf_op jit(solution)/shard_map/ppermute | solution.py:28
  8.8 10.0 %collective-permute-start = (bf16[1552,128]{1,0:T(8,128)(2,1)}, bf16[1552,128]{1,0:T(8,128)(2,1)S(1)}, u32[]{:S(2)}, u32[]{:S(2)}) collective-permute-start(bf16[1552,128]{1,0:T(8,128)(2,1)} %get-tuple-element.25.own_ref), channel_id=1, source_target_pairs={{0,1},{1,0},{2,3},{3,2},{4,5},{5,4},{6,7},{7,6},{8,9},{9,8},{10,11... | collective-permute-start | bytes 1191944 | tf_op jit(solution)/shard_map/ppermute | solution.py:28
  10.1 8.8 %copy-start.3 = (bf16[1552,128]{1,0:T(8,128)(2,1)S(1)}, bf16[1552,128]{1,0:T(8,128)(2,1)}, u32[]{:S(2)}) copy-start(bf16[1552,128]{1,0:T(8,128)(2,1)} %get-tuple-element.25.own_ref) | copy-start | bytes 1191940
  13.5 10.2 %copy-start.1 = (bf16[1,1,3,4,256,256]{5,4,3,2,1,0:T(8,128)(2,1)S(1)}, bf16[1,1,3,4,256,256]{5,4,3,2,1,0:T(8,128)(2,1)}, u32[]{:S(2)}) copy-start(bf16[1,1,3,4,256,256]{5,4,3,2,1,0:T(8,128)(2,1)} %param.7) | copy-start | bytes 4718596
  13.5 10.2 %copy-start.2 = (f32[2,256,256]{2,1,0:T(8,128)S(1)}, f32[2,256,256]{2,1,0:T(8,128)}, u32[]{:S(2)}) copy-start(f32[2,256,256]{2,1,0:T(8,128)} %probe_ref.1) | copy-start | bytes 1572868
  13.5 10.2 %copy-start.4 = (s32[1,1,3,4,2]{3,4,2,1,0:T(2,128)S(1)}, s32[1,1,3,4,2]{3,4,2,1,0:T(2,128)}, u32[]{:S(2)}) copy-start(s32[1,1,3,4,2]{3,4,2,1,0:T(2,128)} %param.8) | copy-start | bytes 292
  13.5 10.2 %copy-start.5 = (s32[1,1,3]{2,1,0:T(1,128)S(1)}, s32[1,1,3]{2,1,0:T(1,128)}, u32[]{:S(2)}) copy-start(s32[1,1,3]{2,1,0:T(1,128)} %refs_1_.3) | copy-start | bytes 40
  19.1 7.2 %collective-permute-start.2 = (bf16[1584,128]{1,0:T(8,128)(2,1)S(1)}, bf16[1584,128]{1,0:T(8,128)(2,1)S(1)}, u32[]{:S(2)}, u32[]{:S(2)}) collective-permute-start(bf16[1584,128]{1,0:T(8,128)(2,1)S(1)} %get-tuple-element.32), channel_id=1, source_target_pairs={{0,8},{8,0},{16,24},{24,16},{32,40},{40,32},{48,56},{56,48},{64,72... | collective-permute-start | bytes 1216520 | tf_op jit(solution)/shard_map/ppermute | solution.py:28
  21.0 11.3 %collective-permute-start.3 = (bf16[1584,128]{1,0:T(8,128)(2,1)S(1)}, bf16[1584,128]{1,0:T(8,128)(2,1)S(1)}, u32[]{:S(2)}, u32[]{:S(2)}) collective-permute-start(bf16[1584,128]{1,0:T(8,128)(2,1)S(1)} %get-tuple-element.33), channel_id=1, source_target_pairs={{8,16},{16,8},{24,32},{32,24},{40,48},{48,40},{56,64},{64,56},{72,... | collective-permute-start | bytes 1216520 | tf_op jit(solution)/shard_map/ppermute | solution.py:28
  35.1 7.1 %collective-permute-start.4 = (bf16[1536,128]{1,0:T(8,128)(2,1)S(1)}, bf16[1536,128]{1,0:T(8,128)(2,1)S(1)}, u32[]{:S(2)}, u32[]{:S(2)}) collective-permute-start(bf16[1536,128]{1,0:T(8,128)(2,1)S(1)} %get-tuple-element.37), channel_id=1, source_target_pairs={{0,8},{8,0},{16,24},{24,16},{32,40},{40,32},{48,56},{56,48},{64,72... | collective-permute-start | bytes 1179656 | tf_op jit(solution)/shard_map/ppermute | solution.py:28
  35.2 11.2 %collective-permute-start.5 = (bf16[1536,128]{1,0:T(8,128)(2,1)S(1)}, bf16[1536,128]{1,0:T(8,128)(2,1)S(1)}, u32[]{:S(2)}, u32[]{:S(2)}) collective-permute-start(bf16[1536,128]{1,0:T(8,128)(2,1)S(1)} %get-tuple-element.38), channel_id=1, source_target_pairs={{8,16},{16,8},{24,32},{32,24},{40,48},{48,40},{56,64},{64,56},{72,... | collective-permute-start | bytes 1179656 | tf_op jit(solution)/shard_map/ppermute | solution.py:28
  46.6 10.1 %collective-permute-start.6 = (bf16[1536,128]{1,0:T(8,128)(2,1)S(1)}, bf16[1536,128]{1,0:T(8,128)(2,1)S(1)}, u32[]{:S(2)}, u32[]{:S(2)}) collective-permute-start(bf16[1536,128]{1,0:T(8,128)(2,1)S(1)} %get-tuple-element.40), channel_id=1, source_target_pairs={{0,1},{1,0},{2,3},{3,2},{4,5},{5,4},{6,7},{7,6},{8,9},{9,8},{10,11... | collective-permute-start | bytes 1179656 | tf_op jit(solution)/shard_map/ppermute | solution.py:28
  48.4 13.0 %collective-permute-start.7 = (bf16[1536,128]{1,0:T(8,128)(2,1)S(1)}, bf16[1536,128]{1,0:T(8,128)(2,1)S(1)}, u32[]{:S(2)}, u32[]{:S(2)}) collective-permute-start(bf16[1536,128]{1,0:T(8,128)(2,1)S(1)} %get-tuple-element.41), channel_id=1, source_target_pairs={{1,2},{2,1},{3,4},{4,3},{5,6},{6,5},{9,10},{10,9},{11,12},{12,11},... | collective-permute-start | bytes 1179656 | tf_op jit(solution)/shard_map/ppermute | solution.py:28

commit v3 on v2

--- a/solution.py
+++ b/solution.py
@@ -57,7 +57,7 @@
     return row.astype(f32).astype(bf16)
 
 
-def edges_kernel(pos_ref, counts_ref, obj_hbm, first_ref, second_ref, low, high, sem):
+def edges_kernel(pos_ref, counts_ref, obj_hbm, first_ref, second_ref, meta_ref, low, high, sem):
     tile_r, tile_c = obj_hbm.shape[1:]
     part = 256
     copies = []
@@ -72,6 +72,7 @@
     meta = meta_rows(pos_ref, counts_ref)
     first_ref[2 * tile_r :, :] = meta
     second_ref[2 * tile_r :, :] = meta
+    meta_ref[...] = meta
     for k in range(2 * tile_r // part):
         copies[2 * k].wait()
         copies[2 * k + 1].wait()
@@ -126,7 +127,7 @@
     tail = 2 * (tiles + 2) * margin
     a = za_ref[2 * tile_r :, :].astype(f32)
     b = zb_ref[2 * tile_r :, :].astype(f32)
-    metas = (jnp.where(right_first, b, a).astype(bf16), own_ref[2 * tile_r :, :], jnp.where(right_first, a, b).astype(bf16))
+    metas = (jnp.where(right_first, b, a).astype(bf16), own_ref[...], jnp.where(right_first, a, b).astype(bf16))
     for k, meta in enumerate(metas):
         rows = slice(tail + PACK * k, tail + PACK * (k + 1))
         ya_ref[rows, :] = meta
@@ -134,10 +135,10 @@
         meta_ref[PACK * k : PACK * (k + 1), :] = meta
 
 
-def slots_kernel(outer, *refs):
-    if outer:
-        (pos_ref, counts_ref, obj_in, canvas_in, ya_ref, yb_ref, probe_ref, amp_ref, fwd_ref, bwd_ref, ext_ref,
-         obj, canvas_ref, ra_ref, rb_ref, todo, prb, xs, hs, er) = refs
+def slots_kernel(kind, *refs):
+    if kind in ("far", "near"):
+        (pos_ref, counts_ref, obj_in, canvas_in, halo_ref, probe_ref, amp_ref, fwd_ref, bwd_ref, ext_ref,
+         obj, canvas_ref, rim_ref, todo, prb, xs, hs, er) = refs
     else:
         (pos_ref, counts_ref, obj, canvas_in, probe_ref, amp_ref, fwd_ref, bwd_ref, ext_ref,
          canvas_ref, todo, prb, xs, hs, er) = refs
@@ -146,20 +147,29 @@
     margin = win // 2
     tiles = obj.shape[1] - 2
     tile_r = obj.shape[2] - 2 * margin
-    lower_first = even("row")
-    for c in range(2 if outer else 0):
-        for t in range(tiles + 2):
-            k = (c * (tiles + 2) + t) * margin
-            a = ya_ref[k : k + margin, :].astype(f32)
-            b = yb_ref[k : k + margin, :].astype(f32)
-            obj[c, t, 0:margin, :] = jnp.where(lower_first, b, a)
-            obj[c, t, margin + tile_r :, :] = jnp.where(lower_first, a, b)
+    tile_c = tiles * LANES
+    upper = even("row") == (kind == "far")
+    place = pl.multiple_of(jnp.where(upper, 0, margin + tile_r), margin)
+    if kind in ("far", "near"):
+        for c in range(2):
+            for t in range(tiles + 2):
+                k = (c * (tiles + 2) + t) * margin
+                obj[c, t, pl.ds(place, margin), :] = halo_ref[k : k + margin, :].astype(f32)
+
+    def member(row, col):
+        inside = (row >= 0) & (row <= tile_r - win)
+        between = (col >= 0) & (col <= tile_c - win)
+        if kind == "core":
+            return inside & between
+        if kind == "inner":
+            return inside & jnp.logical_not(between)
+        return jnp.logical_not(inside) & ((row < 0) == upper)
 
     def collect(slot, count):
         batch = slot // slots
         row = pos_ref[0, 0, batch, 0, slot - batch * slots]
-        inside = (row >= 0) & (row <= tile_r - win)
-        live = (slot - batch * slots < counts_ref[0, 0, batch]) & (inside != outer)
+        col = pos_ref[0, 0, batch, 1, slot - batch * slots]
+        live = (slot - batch * slots < counts_ref[0, 0, batch]) & member(row, col)
 
         @pl.when(live)
         def _():
@@ -268,13 +278,11 @@
 
     lax.fori_loop(0, (total + GROUP - 1) // GROUP, group, 0)
 
-    for c in range(2 if outer else 0):
-        for t in range(tiles + 2):
-            k = (c * (tiles + 2) + t) * margin
-            top = canvas_ref[c, t, 0:margin, :]
-            bottom = canvas_ref[c, t, margin + tile_r :, :]
-            ra_ref[k : k + margin, :] = jnp.where(lower_first, bottom, top).astype(bf16)
-            rb_ref[k : k + margin, :] = jnp.where(lower_first, top, bottom).astype(bf16)
+    if kind in ("far", "near"):
+        for c in range(2):
+            for t in range(tiles + 2):
+                k = (c * (tiles + 2) + t) * margin
+                rim_ref[k : k + margin, :] = canvas_ref[c, t, pl.ds(place, margin), :].astype(bf16)
 
 
 def light_kernel(meta_ref, ya_ref, yb_ref, probe_ref, scale_ref, power, light, rows_ref, table_ref, sem):
@@ -422,15 +430,14 @@
     side = shape((2 * tile_r + PACK, LANES), bf16)
     strip = shape((2 * (tiles + 2) * margin, LANES), bf16)
 
-    za, zb = pl.pallas_call(
+    za, zb, own = pl.pallas_call(
         edges_kernel,
-        out_shape=(side, side),
+        out_shape=(side, side, shape((PACK, LANES), bf16)),
         in_specs=[SMEM, SMEM, ANY],
-        out_specs=(VMEM, VMEM),
+        out_specs=(VMEM,) * 3,
         scratch_shapes=[pltpu.VMEM((2 * tile_r, LANES), f32)] * 2 + [pltpu.SemaphoreType.DMA((2, 2 * tile_r // 256))],
         name="edges",
     )(places, counts, object_field)
-    own = za
     za, zb = swap(za, "col", 0), swap(zb, "col", 1)
     obj, canvas = pl.pallas_call(
         prepare_kernel,
@@ -443,6 +450,32 @@
         name="prepare",
     )(object_field)
     obj, fwd, bwd, ext = lax.optimization_barrier((obj, fwd, bwd, ext))
+    amps = amplitudes.reshape(batches * slots, window, window)
+    tail = (probe, amps, fwd, bwd, ext)
+
+    def run(kind, obj, canvas, *halo):
+        edge = len(halo)
+        big = shape(padded, f32)
+        return pl.pallas_call(
+            functools.partial(slots_kernel, kind),
+            out_shape=(big, big, strip) if edge else big,
+            in_specs=[SMEM, SMEM] + [VMEM] * (7 + edge),
+            out_specs=(VMEM,) * 3 if edge else VMEM,
+            input_output_aliases={2: 0, 3: 1} if edge else {3: 0},
+            scratch_shapes=[
+                pltpu.SMEM((batches * slots,), jnp.int32),
+                pltpu.VMEM((GROUP, 2, 2, window, LANES), f32),
+                pltpu.VMEM((2 * window, GROUP * window), bf16),
+                pltpu.VMEM((GROUP, window, 2 * window), bf16),
+                pltpu.VMEM((GROUP, 2 * window, 2 * window), bf16),
+            ],
+            compiler_params=pltpu.CompilerParams(vmem_limit_bytes=14 << 20),
+            cost_estimate=pl.CostEstimate(flops=2 << 30, bytes_accessed=8 << 20, transcendentals=0),
+            name=kind,
+        )(places, counts, obj, canvas, *halo, *tail)
+
+    canvas = run("core", obj, canvas)
+    obj, canvas, za, zb = lax.optimization_barrier((obj, canvas, za, zb))
     packed = shape((strip.shape[0] + 3 * PACK, LANES), bf16)
     obj, ya, yb, meta = pl.pallas_call(
         sides_kernel,
@@ -453,37 +486,23 @@
         compiler_params=pltpu.CompilerParams(vmem_limit_bytes=4 << 20),
         name="sides",
     )(obj, za, zb, own)
-    ya, yb = swap(ya, "row", 0), swap(yb, "row", 1)
-    amps = amplitudes.reshape(batches * slots, window, window)
-    scratch = [
-        pltpu.SMEM((batches * slots,), jnp.int32),
-        pltpu.VMEM((GROUP, 2, 2, window, LANES), f32),
-        pltpu.VMEM((2 * window, GROUP * window), bf16),
-        pltpu.VMEM((GROUP, window, 2 * window), bf16),
-        pltpu.VMEM((GROUP, 2 * window, 2 * window), bf16),
-    ]
-    canvas = pl.pallas_call(
-        functools.partial(slots_kernel, False),
-        out_shape=shape(padded, f32),
-        in_specs=[SMEM, SMEM] + [VMEM] * 7,
-        out_specs=VMEM,
-        input_output_aliases={3: 0},
-        scratch_shapes=scratch,
-        compiler_params=pltpu.CompilerParams(vmem_limit_bytes=14 << 20),
-        cost_estimate=pl.CostEstimate(flops=4 << 30, bytes_accessed=20 << 20, transcendentals=0),
-        name="inner",
-    )(places, counts, obj, canvas, probe, amps, fwd, bwd, ext)
-    _, canvas, ra, rb = pl.pallas_call(
-        functools.partial(slots_kernel, True),
-        out_shape=(shape(padded, f32), shape(padded, f32), strip, strip),
-        in_specs=[SMEM, SMEM] + [VMEM] * 9,
-        out_specs=(VMEM,) * 4,
-        input_output_aliases={2: 0, 3: 1},
-        scratch_shapes=scratch,
-        compiler_params=pltpu.CompilerParams(vmem_limit_bytes=14 << 20),
-        name="outer",
-    )(places, counts, obj, canvas, ya, yb, probe, amps, fwd, bwd, ext)
-    ra, rb = swap(ra, "row", 0), swap(rb, "row", 1)
+    yb, ya = swap(yb, "row", 1), swap(ya, "row", 0)
+    canvas = run("inner", obj, canvas)
+    obj, canvas, rb = run("far", obj, canvas, yb)
+    rb = swap(rb, "row", 1)
+    obj, canvas, ra = run("near", obj, canvas, ya)
+    ra = swap(ra, "row", 0)
+    rim = shape((2 * tile_r, LANES), bf16)
+    sa, sb = pl.pallas_call(
+        strips_kernel,
+        out_shape=(rim, rim),
+        in_specs=[VMEM] * 3,
+        out_specs=(VMEM, VMEM),
+        compiler_params=pltpu.CompilerParams(vmem_limit_bytes=4 << 20),
+        name="strips",
+    )(canvas, ra, rb)
+    sa, sb, probe = lax.optimization_barrier((sa, sb, probe))
+    sa, sb = swap(sa, "col", 0), swap(sb, "col", 1)
     scale = pl.pallas_call(
         light_kernel,
         out_shape=shape((tiles, tile_r, LANES), f32),
@@ -500,17 +519,6 @@
         cost_estimate=pl.CostEstimate(flops=8 << 20, bytes_accessed=12 << 20, transcendentals=0),
         name="light",
     )(meta, ya, yb, probe)
-    canvas, scale = lax.optimization_barrier((canvas, scale))
-    rim = shape((2 * tile_r, LANES), bf16)
-    sa, sb = pl.pallas_call(
-        strips_kernel,
-        out_shape=(rim, rim),
-        in_specs=[VMEM] * 3,
-        out_specs=(VMEM, VMEM),
-        compiler_params=pltpu.CompilerParams(vmem_limit_bytes=4 << 20),
-        name="strips",
-    )(canvas, ra, rb)
-    sa, sb = swap(sa, "col", 0), swap(sb, "col", 1)
     field = shape((2, tile_r, tile_c), f32)
 
     def update(outer, aliases, *args):

time: 64.5 us -> 61.3 us (0.950); the launches traced: 63.3 us -> 61.3 us
  waiting for transfers between devices: 23.8 us -> 14.6 us
  Pallas kernels: 18.1 us -> 22.3 us
  starting transfers between devices: 17 us -> 19.9 us
    ppermute x8, waiting for transfers between devices: 23.8 us -> 14.6 us  [swap(): return lax.ppermute(block, axis, route)]
    pallas_call x3 -> x5, Pallas kernels: 8.65 us -> 12.4 us  [the longest x4 9.03 us: run(): pl.pallas_call(functools.partial(slots_kernel, kind), out_shape=(big, big...]
    ppermute x8, starting transfers between devices: 17 us -> 19.9 us  [swap(): return lax.ppermute(block, axis, route)]
  transfers between devices with their start and end apart: 8 -> 8, of which waited for: 6 -> 4; matrix products, arithmetic and copies ran while one was open for 5% -> 6% of each run, Pallas kernels for 15% -> 27%
where the time goes in v3:
time: 61.3 us
  Pallas kernels  22.3 us (36%)
  starting transfers between devices  19.9 us (32%)
  waiting for transfers between devices  14.6 us (24%)
  other arithmetic  3.39 us (6%)
  between operations  1.08 us (2%)
    ppermute x8, starting transfers between devices, swap(): return lax.ppermute(block, axis, route)  19.9 us
    ppermute x8, waiting for transfers between devices, swap(): return lax.ppermute(block, axis, route)  14.6 us
    pallas_call x4, Pallas kernels, run(): pl.pallas_call(functools.partial(slots_kernel, kind), out_shape=(big, big...  9.03 us
    pallas_call x1, Pallas kernels, on_device(): pl.pallas_call(light_kernel, out_shape=shape((tiles, tile_r, LANES), f32)...  4.65 us
    pallas_call x2, Pallas kernels, update(): pl.pallas_call(functools.partial(update_kernel, outer), out_shape=(field,...  3.68 us
    pallas_call x1, Pallas kernels, on_device(): pl.pallas_call(edges_kernel, out_shape=(side, side, shape((PACK, LANES),...  3.39 us
  transfers between devices with their start and end apart: 8, of which 4 were waited for; matrix products, arithmetic and copies ran while one was open for 6% of the time, Pallas kernels for 27%

profile of v3, /device:TPU:123, one launch (start us, length us, event | category | flops | bytes accessed | tf_op | source)
XLA Modules:
  0.0 61.3 jit_solution(10058676783617901720)
XLA Ops:
  0.7 3.4 %edges.1 = (bf16[1552,128]{1,0:T(8,128)(2,1)}, bf16[1552,128]{1,0:T(8,128)(2,1)}, bf16[16,128]{1,0:T(8,128)(2,1)}) custom-call(s32[1,1,3,2,4]{4,3,2,1,0:T(2,128)} %bitcast.8, s32[1,1,3]{2,1,0:T(1,128)} %refs_1_.7, f32[2,768,512]{2,1,0:T(8,128)} %refs_0_.3), custom_call_target="tpu_custom_call" | custom-call | tf_op jit(solution)/shard_map/edges/pallas_call | solution.py:433
  4.1 0.0 copy-start.1
  4.1 0.0 copy-start.2
  4.1 0.1 collective-permute-start
  4.2 5.5 %collective-permute-start.1 = (bf16[1552,128]{1,0:T(8,128)(2,1)}, bf16[1552,128]{1,0:T(8,128)(2,1)S(1)}, u32[]{:S(2)}, u32[]{:S(2)}) collective-permute-start(bf16[1552,128]{1,0:T(8,128)(2,1)} %get-tuple-element.38), channel_id=1, source_target_pairs={{1,2},{2,1},{3,4},{4,3},{5,6},{6,5},{9,10},{10,9},{11,12},{12,11},... | collective-permute-start | bytes 1191944 | tf_op jit(solution)/shard_map/ppermute | solution.py:28
  9.7 1.1 %multiply_convert_fusion.2 = (bf16[256,256]{1,0:T(8,128)(2,1)S(1)}, bf16[256,256]{1,0:T(8,128)(2,1)S(1)}) fusion(), kind=kLoop, calls=%fused_computation.23 | loop fusion | flops 1245184 | bytes 262144 | tf_op jit(solution)/shard_map/convert_element_type | solution.py:42
  10.8 1.1 %multiply_convert_fusion.1 = (bf16[1,256,2,128]{3,1,2,0:T(8,128)(2,1)S(1)}, bf16[1,256,2,128]{3,1,2,0:T(8,128)(2,1)S(1)}) fusion(s32[2,128]{1,0:T(2,128)S(1)} %multiply_add_fusion), kind=kLoop, calls=%fused_computation.20 | loop fusion | flops 1245184 | bytes 263168 | tf_op jit(solution)/shard_map/convert_element_type | solution.py:41
  11.9 0.1 convert_bitcast_fusion.refs_8_.refs_9_
  12.0 1.0 %fusion.14 = bf16[256,256]{1,0:T(8,128)(2,1)S(1)} fusion(), kind=kLoop, calls=%fused_computation.29 | loop fusion | flops 1310720 | bytes 131072 | tf_op jit(solution)/shard_map/neg | solution.py:424
  13.0 1.1 %prepare.1 = (f32[2,6,1024,128]{3,2,1,0:T(8,128)S(1)}, f32[2,6,1024,128]{3,2,1,0:T(8,128)S(1)}) custom-call(f32[2,768,512]{2,1,0:T(8,128)S(1)} %copy-done), custom_call_target="tpu_custom_call" | custom-call | flops 4194304 | bytes 16777216 | tf_op jit(solution)/shard_map/prepare/pallas_call | solution.py:442
  14.2 0.1 fusion.1
  14.3 0.9 %core.1.refs_3_ = f32[2,6,1024,128]{3,2,1,0:T(8,128)S(1)} custom-call(s32[1,1,3,2,4]{4,3,2,1,0:T(2,128)S(1)} %bitcast.9, s32[1,1,3]{2,1,0:T(1,128)S(1)} %copy-done.4, f32[2,6,1024,128]{3,2,1,0:T(8,128)S(1)} %get-tuple-element.39.refs_2_.obj_in, f32[2,6,1024,128]{3,2,1,0:T(8,128)S(1)} %get-tuple-element.33.refs_3_, ...), custom_call_target="tpu_custom_call", output_to_operand_aliasing={{}: (3, {})} | custom-call | flops 2147483648 | bytes 8388608 | tf_op jit(solution)/shard_map/core/pallas_call | solution.py:459
  15.2 3.3 %collective-permute-done.1.zb_ref = bf16[1552,128]{1,0:T(8,128)(2,1)S(1)} collective-permute-done((bf16[1552,128]{1,0:T(8,128)(2,1)}, bf16[1552,128]{1,0:T(8,128)(2,1)S(1)}, u32[]{:S(2)}, u32[]{:S(2)}) %collective-permute-start.1) | collective-permute-done | bytes 397344 | tf_op jit(solution)/shard_map/ppermute | solution.py:28
  18.5 0.2 sides.1
  18.7 4.2 %collective-permute-start.2 = (bf16[1584,128]{1,0:T(8,128)(2,1)S(1)}, bf16[1584,128]{1,0:T(8,128)(2,1)S(1)}, u32[]{:S(2)}, u32[]{:S(2)}) collective-permute-start(bf16[1584,128]{1,0:T(8,128)(2,1)S(1)} %get-tuple-element.45), channel_id=1, source_target_pairs={{8,16},{16,8},{24,32},{32,24},{40,48},{48,40},{56,64},{64,56},{72,... | collective-permute-start | bytes 1216520 | tf_op jit(solution)/shard_map/ppermute | solution.py:28
  22.9 0.1 collective-permute-start.3
  23.0 2.6 %inner.1.refs_3_ = f32[2,6,1024,128]{3,2,1,0:T(8,128)S(1)} custom-call(s32[1,1,3,2,4]{4,3,2,1,0:T(2,128)S(1)} %bitcast.10, s32[1,1,3]{2,1,0:T(1,128)S(1)} %copy-done.4, f32[2,6,1024,128]{3,2,1,0:T(8,128)S(1)} %get-tuple-element.43.refs_2_, f32[2,6,1024,128]{3,2,1,0:T(8,128)S(1)} %core.1.refs_3_, ...), custom_call_target="tpu_custom_call", output_to_operand_aliasing={{}: (3, {})} | custom-call | flops 2147483648 | bytes 8388608 | tf_op jit(solution)/shard_map/inner/pallas_call | solution.py:459
  25.6 4.4 %collective-permute-done.2.refs_4_.yb_ref = bf16[1584,128]{1,0:T(8,128)(2,1)S(1)} collective-permute-done((bf16[1584,128]{1,0:T(8,128)(2,1)S(1)}, bf16[1584,128]{1,0:T(8,128)(2,1)S(1)}, u32[]{:S(2)}, u32[]{:S(2)}) %collective-permute-start.2) | collective-permute-done | bytes 405536 | tf_op jit(solution)/shard_map/ppermute | solution.py:28
  30.0 2.7 %far.1 = (f32[2,6,1024,128]{3,2,1,0:T(8,128)S(1)}, f32[2,6,1024,128]{3,2,1,0:T(8,128)S(1)}, bf16[1536,128]{1,0:T(8,128)(2,1)S(1)}) custom-call(s32[1,1,3,2,4]{4,3,2,1,0:T(2,128)S(1)} %bitcast.11, s32[1,1,3]{2,1,0:T(1,128)S(1)} %copy-done.4, f32[2,6,1024,128]{3,2,1,0:T(8,128)S(1)} %get-tuple-element.43.refs_2_, ...), custom_call_target="tpu_custom_call", output_to_operand_aliasing={{0}: (2, {}), {1}: (3, {})} | custom-call | flops 2147483648 | bytes 8388608 | tf_op jit(solution)/shard_map/far/pallas_call | solution.py:459
  32.7 4.2 %collective-permute-start.5 = (bf16[1536,128]{1,0:T(8,128)(2,1)S(1)}, bf16[1536,128]{1,0:T(8,128)(2,1)S(1)}, u32[]{:S(2)}, u32[]{:S(2)}) collective-permute-start(bf16[1536,128]{1,0:T(8,128)(2,1)S(1)} %get-tuple-element.51), channel_id=1, source_target_pairs={{8,16},{16,8},{24,32},{32,24},{40,48},{48,40},{56,64},{64,56},{72,... | collective-permute-start | bytes 1179656 | tf_op jit(solution)/shard_map/ppermute | solution.py:28
  36.9 0.0 collective-permute-done.3.refs_4_.ya_ref
  36.9 2.9 %near.1 = (f32[2,6,1024,128]{3,2,1,0:T(8,128)S(1)}, f32[2,6,1024,128]{3,2,1,0:T(8,128)S(1)}, bf16[1536,128]{1,0:T(8,128)(2,1)S(1)}) custom-call(s32[1,1,3,2,4]{4,3,2,1,0:T(2,128)S(1)} %bitcast.12, s32[1,1,3]{2,1,0:T(1,128)S(1)} %copy-done.4, f32[2,6,1024,128]{3,2,1,0:T(8,128)S(1)} %get-tuple-element.46.refs_2_, ...), custom_call_target="tpu_custom_call", output_to_operand_aliasing={{0}: (2, {}), {1}: (3, {})} | custom-call | flops 2147483648 | bytes 8388608 | tf_op jit(solution)/shard_map/near/pallas_call | solution.py:459
  39.8 0.1 collective-permute-start.4
  39.9 4.0 %collective-permute-done.5.yb_ref.refs_3_ = bf16[1536,128]{1,0:T(8,128)(2,1)S(1)} collective-permute-done((bf16[1536,128]{1,0:T(8,128)(2,1)S(1)}, bf16[1536,128]{1,0:T(8,128)(2,1)S(1)}, u32[]{:S(2)}, u32[]{:S(2)}) %collective-permute-start.5) | collective-permute-done | bytes 393248 | tf_op jit(solution)/shard_map/ppermute | solution.py:28
  43.9 0.0 collective-permute-done.4.ya_ref.refs_2_
  43.9 0.2 strips.1
  44.1 0.1 collective-permute-start.6
  44.2 5.7 %collective-permute-start.7 = (bf16[1536,128]{1,0:T(8,128)(2,1)S(1)}, bf16[1536,128]{1,0:T(8,128)(2,1)S(1)}, u32[]{:S(2)}, u32[]{:S(2)}) collective-permute-start(bf16[1536,128]{1,0:T(8,128)(2,1)S(1)} %get-tuple-element.57), channel_id=1, source_target_pairs={{1,2},{2,1},{3,4},{4,3},{5,6},{6,5},{9,10},{10,9},{11,12},{12,11},... | collective-permute-start | bytes 1179656 | tf_op jit(solution)/shard_map/ppermute | solution.py:28
  49.9 4.6 %light.1.refs_4_ = f32[4,768,128]{2,1,0:T(8,128)S(1)} custom-call(bf16[48,128]{1,0:T(8,128)(2,1)S(1)} %get-tuple-element.52.meta_ref, bf16[1584,128]{1,0:T(8,128)(2,1)S(1)} %collective-permute-done.3.refs_4_.ya_ref, bf16[1584,128]{1,0:T(8,128)(2,1)S(1)} %collective-permute-done.2.refs_4_.yb_ref, f32[2,256,256]{2,1,0:T(8,128)S(1)} %copy-done.2), custom_call_target="tpu_custom_call" | custom-call | flops 8388608 | bytes 12582912 | tf_op jit(solution)/shard_map/light/pallas_call | solution.py:506
  54.5 1.8 %middle.1 = (f32[2,768,512]{2,1,0:T(8,128)}, f32[2,768,512]{2,1,0:T(8,128)}) custom-call(f32[2,768,512]{2,1,0:T(8,128)S(1)} %copy-done, f32[2,6,1024,128]{3,2,1,0:T(8,128)S(1)} %get-tuple-element.49.canvas_ref.refs_1_, bf16[1536,128]{1,0:T(8,128)(2,1)S(1)} %collective-permute-done.4.ya_ref.refs_2_, ...), custom_call_target="tpu_custom_call" | custom-call | flops 4194304 | bytes 10485760 | tf_op jit(solution)/shard_map/middle/pallas_call | solution.py:525
  56.4 2.8 %collective-permute-done.7.refs_6_ = bf16[1536,128]{1,0:T(8,128)(2,1)S(1)} collective-permute-done((bf16[1536,128]{1,0:T(8,128)(2,1)S(1)}, bf16[1536,128]{1,0:T(8,128)(2,1)S(1)}, u32[]{:S(2)}, u32[]{:S(2)}) %collective-permute-start.7) | collective-permute-done | bytes 393248 | tf_op jit(solution)/shard_map/ppermute | solution.py:28
  59.2 1.9 %rims.1 = (f32[2,768,512]{2,1,0:T(8,128)}, f32[2,768,512]{2,1,0:T(8,128)}) custom-call(f32[2,768,512]{2,1,0:T(8,128)S(1)} %copy-done, f32[2,6,1024,128]{3,2,1,0:T(8,128)S(1)} %get-tuple-element.49.canvas_ref.refs_1_, bf16[1536,128]{1,0:T(8,128)(2,1)S(1)} %collective-permute-done.4.ya_ref.refs_2_, ...), custom_call_target="tpu_custom_call", output_to_operand_aliasing={{0}: (7, {}), {1}: (8, {})} | custom-call | flops 4194304 | bytes 10485760 | tf_op jit(solution)/shard_map/rims/pallas_call | solution.py:525
  (13 shorter events, 0.0 us)
Async XLA Ops:
  0.6 13.6 %copy-start.4 = (s32[1,1,3]{2,1,0:T(1,128)S(1)}, s32[1,1,3]{2,1,0:T(1,128)}, u32[]{:S(2)}) copy-start(s32[1,1,3]{2,1,0:T(1,128)} %refs_1_.7) | copy-start | bytes 40
  0.6 12.4 %copy-start = (f32[2,768,512]{2,1,0:T(8,128)S(1)}, f32[2,768,512]{2,1,0:T(8,128)}, u32[]{:S(2)}) copy-start(f32[2,768,512]{2,1,0:T(8,128)} %refs_0_.3) | copy-start | bytes 9437188
  0.6 13.6 %copy-start.3 = (s32[1,1,3,4,2]{3,4,2,1,0:T(2,128)S(1)}, s32[1,1,3,4,2]{3,4,2,1,0:T(2,128)}, u32[]{:S(2)}) copy-start(s32[1,1,3,4,2]{3,4,2,1,0:T(2,128)} %param.8) | copy-start | bytes 292
  4.1 10.2 %copy-start.1 = (bf16[1,1,3,4,256,256]{5,4,3,2,1,0:T(8,128)(2,1)S(1)}, bf16[1,1,3,4,256,256]{5,4,3,2,1,0:T(8,128)(2,1)}, u32[]{:S(2)}) copy-start(bf16[1,1,3,4,256,256]{5,4,3,2,1,0:T(8,128)(2,1)} %param.7) | copy-start | bytes 4718596
  4.1 10.2 %copy-start.2 = (f32[2,256,256]{2,1,0:T(8,128)S(1)}, f32[2,256,256]{2,1,0:T(8,128)}, u32[]{:S(2)}) copy-start(f32[2,256,256]{2,1,0:T(8,128)} %probe_ref) | copy-start | bytes 1572868
  4.1 11.1 %collective-permute-start = (bf16[1552,128]{1,0:T(8,128)(2,1)}, bf16[1552,128]{1,0:T(8,128)(2,1)S(1)}, u32[]{:S(2)}, u32[]{:S(2)}) collective-permute-start(bf16[1552,128]{1,0:T(8,128)(2,1)} %get-tuple-element.37), channel_id=1, source_target_pairs={{0,1},{1,0},{2,3},{3,2},{4,5},{5,4},{6,7},{7,6},{8,9},{9,8},{10,11... | collective-permute-start | bytes 1191944 | tf_op jit(solution)/shard_map/ppermute | solution.py:28
  4.2 14.3 %collective-permute-start.1 = (bf16[1552,128]{1,0:T(8,128)(2,1)}, bf16[1552,128]{1,0:T(8,128)(2,1)S(1)}, u32[]{:S(2)}, u32[]{:S(2)}) collective-permute-start(bf16[1552,128]{1,0:T(8,128)(2,1)} %get-tuple-element.38), channel_id=1, source_target_pairs={{1,2},{2,1},{3,4},{4,3},{5,6},{6,5},{9,10},{10,9},{11,12},{12,11},... | collective-permute-start | bytes 1191944 | tf_op jit(solution)/shard_map/ppermute | solution.py:28
  14.3 4.2 %copy-start.5 = (bf16[16,128]{1,0:T(8,128)(2,1)S(1)}, bf16[16,128]{1,0:T(8,128)(2,1)}, u32[]{:S(2)}) copy-start(bf16[16,128]{1,0:T(8,128)(2,1)} %get-tuple-element.42.own_ref) | copy-start | bytes 12292
  18.7 11.3 %collective-permute-start.2 = (bf16[1584,128]{1,0:T(8,128)(2,1)S(1)}, bf16[1584,128]{1,0:T(8,128)(2,1)S(1)}, u32[]{:S(2)}, u32[]{:S(2)}) collective-permute-start(bf16[1584,128]{1,0:T(8,128)(2,1)S(1)} %get-tuple-element.45), channel_id=1, source_target_pairs={{8,16},{16,8},{24,32},{32,24},{40,48},{48,40},{56,64},{64,56},{72,... | collective-permute-start | bytes 1216520 | tf_op jit(solution)/shard_map/ppermute | solution.py:28
  22.9 14.0 %collective-permute-start.3 = (bf16[1584,128]{1,0:T(8,128)(2,1)S(1)}, bf16[1584,128]{1,0:T(8,128)(2,1)S(1)}, u32[]{:S(2)}, u32[]{:S(2)}) collective-permute-start(bf16[1584,128]{1,0:T(8,128)(2,1)S(1)} %get-tuple-element.48), channel_id=1, source_target_pairs={{0,8},{8,0},{16,24},{24,16},{32,40},{40,32},{48,56},{56,48},{64,72... | collective-permute-start | bytes 1216520 | tf_op jit(solution)/shard_map/ppermute | solution.py:28
  32.7 11.2 %collective-permute-start.5 = (bf16[1536,128]{1,0:T(8,128)(2,1)S(1)}, bf16[1536,128]{1,0:T(8,128)(2,1)S(1)}, u32[]{:S(2)}, u32[]{:S(2)}) collective-permute-start(bf16[1536,128]{1,0:T(8,128)(2,1)S(1)} %get-tuple-element.51), channel_id=1, source_target_pairs={{8,16},{16,8},{24,32},{32,24},{40,48},{48,40},{56,64},{64,56},{72,... | collective-permute-start | bytes 1179656 | tf_op jit(solution)/shard_map/ppermute | solution.py:28
  39.8 4.1 %collective-permute-start.4 = (bf16[1536,128]{1,0:T(8,128)(2,1)S(1)}, bf16[1536,128]{1,0:T(8,128)(2,1)S(1)}, u32[]{:S(2)}, u32[]{:S(2)}) collective-permute-start(bf16[1536,128]{1,0:T(8,128)(2,1)S(1)} %get-tuple-element.50), channel_id=1, source_target_pairs={{0,8},{8,0},{16,24},{24,16},{32,40},{40,32},{48,56},{56,48},{64,72... | collective-permute-start | bytes 1179656 | tf_op jit(solution)/shard_map/ppermute | solution.py:28
  44.1 12.3 %collective-permute-start.6 = (bf16[1536,128]{1,0:T(8,128)(2,1)S(1)}, bf16[1536,128]{1,0:T(8,128)(2,1)S(1)}, u32[]{:S(2)}, u32[]{:S(2)}) collective-permute-start(bf16[1536,128]{1,0:T(8,128)(2,1)S(1)} %get-tuple-element.56), channel_id=1, source_target_pairs={{0,1},{1,0},{2,3},{3,2},{4,5},{5,4},{6,7},{7,6},{8,9},{9,8},{10,11... | collective-permute-start | bytes 1179656 | tf_op jit(solution)/shard_map/ppermute | solution.py:28
  44.2 15.0 %collective-permute-start.7 = (bf16[1536,128]{1,0:T(8,128)(2,1)S(1)}, bf16[1536,128]{1,0:T(8,128)(2,1)S(1)}, u32[]{:S(2)}, u32[]{:S(2)}) collective-permute-start(bf16[1536,128]{1,0:T(8,128)(2,1)S(1)} %get-tuple-element.57), channel_id=1, source_target_pairs={{1,2},{2,1},{3,4},{4,3},{5,6},{6,5},{9,10},{10,9},{11,12},{12,11},... | collective-permute-start | bytes 1179656 | tf_op jit(solution)/shard_map/ppermute | solution.py:28

commit v4 on v3

--- a/solution.py
+++ b/solution.py
@@ -180,20 +180,19 @@
     total = lax.fori_loop(0, batches * slots, collect, jnp.int32(0))
     lane = lax.broadcasted_iota(jnp.int32, (CHUNK, LANES), 1)
 
-    def group(p, carry):
+    def group(first, width):
         chosen = []
-        for g in range(GROUP):
-            at = p * GROUP + g
-            slot = todo[jnp.minimum(at, total - 1)]
+        for g in range(width):
+            slot = todo[first + g]
             batch = slot // slots
             row = pos_ref[0, 0, batch, 0, slot - batch * slots] + margin
             col = pos_ref[0, 0, batch, 1, slot - batch * slots] + margin
             tile = col // LANES
             shift = col - tile * LANES
-            chosen.append((slot, row, tile, jnp.minimum(tile + 2, tiles + 1), shift, at < total))
+            chosen.append((slot, row, tile, jnp.minimum(tile + 2, tiles + 1), shift))
 
         def exit_waves(g):
-            slot, row, tile, wrapped, shift, valid = chosen[g]
+            slot, row, tile, wrapped, shift = chosen[g]
             low = lane < shift
             for i in range(0, win, CHUNK):
                 turned = []
@@ -229,7 +228,7 @@
                     er[g, win + i : win + i + CHUNK, b] = real
 
         def rows_dft(table_ref):
-            for g in range(GROUP):
+            for g in range(width):
                 for part in range(2):
                     out = jnp.dot(
                         table_ref[win * part : win * (part + 1), :],
@@ -246,7 +245,7 @@
             xs[win:, win * g : win * (g + 1)] = (imag * scale).astype(bf16)
 
         def accumulate(g):
-            slot, row, tile, wrapped, shift, valid = chosen[g]
+            slot, row, tile, wrapped, shift = chosen[g]
             back = lax.dot_general(hs[g], er[g], (((1,), (1,)), ((), ())), preferred_element_type=f32)
             keep = lax.broadcasted_iota(jnp.int32, (win, LANES), 1) < shift
             at = pl.ds(row, win)
@@ -255,8 +254,6 @@
                 br = back[:, LANES * h : LANES * (h + 1)]
                 bi = back[:, win + LANES * h : win + LANES * (h + 1)]
                 terms = [pr * br + pi * bi, pr * bi - pi * br]
-                if g:
-                    terms = [jnp.where(valid, term, 0.0) for term in terms]
                 for c in range(2):
                     if h == 0:
                         canvas_ref[c, tile, at, :] += jnp.where(keep, 0.0, terms[c])
@@ -264,19 +261,26 @@
                     else:
                         canvas_ref[c, tile + 1, at, :] += terms[c]
 
-        for g in range(GROUP):
+        for g in range(width):
             exit_waves(g)
         rows_dft(fwd_ref)
-        for g in range(GROUP):
+        for g in range(width):
             rolled_table(g)
-        for g in range(GROUP):
+        for g in range(width):
             residual_waves(g)
         rows_dft(bwd_ref)
-        for g in range(GROUP):
+        for g in range(width):
             accumulate(g)
+
+    def full_group(p, carry):
+        group(p * GROUP, GROUP)
         return carry
 
-    lax.fori_loop(0, (total + GROUP - 1) // GROUP, group, 0)
+    lax.fori_loop(0, total // GROUP, full_group, 0)
+
+    @pl.when(lax.rem(total, GROUP) == 1)
+    def _():
+        group(total - 1, 1)
 
     if kind in ("far", "near"):
         for c in range(2):

time: 61.3 us -> 60.5 us (0.987); the launches traced: 61.3 us -> 59.4 us
  Pallas kernels: 22.3 us -> 19.7 us
  waiting for transfers between devices: 14.6 us -> 16.4 us
  starting transfers between devices: 19.9 us -> 18.8 us
    pallas_call x4, Pallas kernels: 9.03 us -> 7.01 us  [run(): pl.pallas_call(functools.partial(slots_kernel, kind), out_shape=(big, big...]
    ppermute x8, waiting for transfers between devices: 14.6 us -> 16.4 us  [swap(): return lax.ppermute(block, axis, route)]
    ppermute x8, starting transfers between devices: 19.9 us -> 18.8 us  [swap(): return lax.ppermute(block, axis, route)]
  transfers between devices with their start and end apart: 8 -> 8, of which waited for: 4 -> 4; matrix products, arithmetic and copies ran while one was open for 6% -> 6% of each run, Pallas kernels for 27% -> 24%
where the time goes in v4:
time: 60.5 us; the launch traced here: 59.4 us
  Pallas kernels  19.7 us (33%)
  starting transfers between devices  18.8 us (31%)
  waiting for transfers between devices  16.4 us (27%)
  other arithmetic  3.39 us (6%)
  between operations  1.08 us (2%)
    ppermute x8, starting transfers between devices, swap(): return lax.ppermute(block, axis, route)  18.8 us
    ppermute x8, waiting for transfers between devices, swap(): return lax.ppermute(block, axis, route)  16.4 us
    pallas_call x4, Pallas kernels, run(): pl.pallas_call(functools.partial(slots_kernel, kind), out_shape=(big, big...  7.01 us
    pallas_call x1, Pallas kernels, on_device(): pl.pallas_call(light_kernel, out_shape=shape((tiles, tile_r, LANES), f32)...  4.06 us
    pallas_call x2, Pallas kernels, update(): pl.pallas_call(functools.partial(update_kernel, outer), out_shape=(field,...  3.68 us
    pallas_call x1, Pallas kernels, on_device(): pl.pallas_call(edges_kernel, out_shape=(side, side, shape((PACK, LANES),...  3.39 us
  transfers between devices with their start and end apart: 8, of which 4 were waited for; matrix products, arithmetic and copies ran while one was open for 6% of the time, Pallas kernels for 24%

profile of v4, /device:TPU:123, one launch (start us, length us, event | category | flops | bytes accessed | tf_op | source)
XLA Modules:
  0.0 59.4 jit_solution(8166567645613696348)
XLA Ops:
  0.7 3.4 %edges.1 = (bf16[1552,128]{1,0:T(8,128)(2,1)}, bf16[1552,128]{1,0:T(8,128)(2,1)}, bf16[16,128]{1,0:T(8,128)(2,1)}) custom-call(s32[1,1,3,2,4]{4,3,2,1,0:T(2,128)} %bitcast.8, s32[1,1,3]{2,1,0:T(1,128)} %refs_1_.7, f32[2,768,512]{2,1,0:T(8,128)} %refs_0_.3), custom_call_target="tpu_custom_call" | custom-call | tf_op jit(solution)/shard_map/edges/pallas_call | solution.py:437
  4.1 0.0 copy-start.1
  4.1 0.0 copy-start.2
  4.1 0.1 collective-permute-start
  4.2 5.5 %collective-permute-start.1 = (bf16[1552,128]{1,0:T(8,128)(2,1)}, bf16[1552,128]{1,0:T(8,128)(2,1)S(1)}, u32[]{:S(2)}, u32[]{:S(2)}) collective-permute-start(bf16[1552,128]{1,0:T(8,128)(2,1)} %get-tuple-element.38), channel_id=1, source_target_pairs={{1,2},{2,1},{3,4},{4,3},{5,6},{6,5},{9,10},{10,9},{11,12},{12,11},... | collective-permute-start | bytes 1191944 | tf_op jit(solution)/shard_map/ppermute | solution.py:28
  9.7 1.1 %multiply_convert_fusion.2 = (bf16[256,256]{1,0:T(8,128)(2,1)S(1)}, bf16[256,256]{1,0:T(8,128)(2,1)S(1)}) fusion(), kind=kLoop, calls=%fused_computation.23 | loop fusion | flops 1245184 | bytes 262144 | tf_op jit(solution)/shard_map/convert_element_type | solution.py:42
  10.8 1.1 %multiply_convert_fusion.1 = (bf16[1,256,2,128]{3,1,2,0:T(8,128)(2,1)S(1)}, bf16[1,256,2,128]{3,1,2,0:T(8,128)(2,1)S(1)}) fusion(s32[2,128]{1,0:T(2,128)S(1)} %multiply_add_fusion), kind=kLoop, calls=%fused_computation.20 | loop fusion | flops 1245184 | bytes 263168 | tf_op jit(solution)/shard_map/convert_element_type | solution.py:41
  11.9 0.1 convert_bitcast_fusion.refs_8_.refs_9_
  12.0 1.0 %fusion.14 = bf16[256,256]{1,0:T(8,128)(2,1)S(1)} fusion(), kind=kLoop, calls=%fused_computation.29 | loop fusion | flops 1310720 | bytes 131072 | tf_op jit(solution)/shard_map/neg | solution.py:428
  13.0 1.1 %prepare.1 = (f32[2,6,1024,128]{3,2,1,0:T(8,128)S(1)}, f32[2,6,1024,128]{3,2,1,0:T(8,128)S(1)}) custom-call(f32[2,768,512]{2,1,0:T(8,128)S(1)} %copy-done), custom_call_target="tpu_custom_call" | custom-call | flops 4194304 | bytes 16777216 | tf_op jit(solution)/shard_map/prepare/pallas_call | solution.py:446
  14.2 0.1 fusion.1
  14.3 0.9 %core.1.refs_3_ = f32[2,6,1024,128]{3,2,1,0:T(8,128)S(1)} custom-call(s32[1,1,3,2,4]{4,3,2,1,0:T(2,128)S(1)} %bitcast.9, s32[1,1,3]{2,1,0:T(1,128)S(1)} %copy-done.4, f32[2,6,1024,128]{3,2,1,0:T(8,128)S(1)} %get-tuple-element.39.refs_2_.obj_in, f32[2,6,1024,128]{3,2,1,0:T(8,128)S(1)} %get-tuple-element.33.refs_3_, ...), custom_call_target="tpu_custom_call", output_to_operand_aliasing={{}: (3, {})} | custom-call | flops 2147483648 | bytes 8388608 | tf_op jit(solution)/shard_map/core/pallas_call | solution.py:463
  15.2 0.0 collective-permute-done.za_ref
  15.2 3.3 %collective-permute-done.1.zb_ref = bf16[1552,128]{1,0:T(8,128)(2,1)S(1)} collective-permute-done((bf16[1552,128]{1,0:T(8,128)(2,1)}, bf16[1552,128]{1,0:T(8,128)(2,1)S(1)}, u32[]{:S(2)}, u32[]{:S(2)}) %collective-permute-start.1) | collective-permute-done | bytes 397344 | tf_op jit(solution)/shard_map/ppermute | solution.py:28
  18.5 0.2 sides.1
  18.7 4.2 %collective-permute-start.2 = (bf16[1584,128]{1,0:T(8,128)(2,1)S(1)}, bf16[1584,128]{1,0:T(8,128)(2,1)S(1)}, u32[]{:S(2)}, u32[]{:S(2)}) collective-permute-start(bf16[1584,128]{1,0:T(8,128)(2,1)S(1)} %get-tuple-element.45), channel_id=1, source_target_pairs={{8,16},{16,8},{24,32},{32,24},{40,48},{48,40},{56,64},{64,56},{72,... | collective-permute-start | bytes 1216520 | tf_op jit(solution)/shard_map/ppermute | solution.py:28
  22.9 0.1 collective-permute-start.3
  23.0 0.9 %inner.1.refs_3_ = f32[2,6,1024,128]{3,2,1,0:T(8,128)S(1)} custom-call(s32[1,1,3,2,4]{4,3,2,1,0:T(2,128)S(1)} %bitcast.10, s32[1,1,3]{2,1,0:T(1,128)S(1)} %copy-done.4, f32[2,6,1024,128]{3,2,1,0:T(8,128)S(1)} %get-tuple-element.43.refs_2_, f32[2,6,1024,128]{3,2,1,0:T(8,128)S(1)} %core.1.refs_3_, ...), custom_call_target="tpu_custom_call", output_to_operand_aliasing={{}: (3, {})} | custom-call | flops 2147483648 | bytes 8388608 | tf_op jit(solution)/shard_map/inner/pallas_call | solution.py:463
  23.9 6.1 %collective-permute-done.2.refs_4_.yb_ref = bf16[1584,128]{1,0:T(8,128)(2,1)S(1)} collective-permute-done((bf16[1584,128]{1,0:T(8,128)(2,1)S(1)}, bf16[1584,128]{1,0:T(8,128)(2,1)S(1)}, u32[]{:S(2)}, u32[]{:S(2)}) %collective-permute-start.2) | collective-permute-done | bytes 405536 | tf_op jit(solution)/shard_map/ppermute | solution.py:28
  30.0 2.5 %far.1 = (f32[2,6,1024,128]{3,2,1,0:T(8,128)S(1)}, f32[2,6,1024,128]{3,2,1,0:T(8,128)S(1)}, bf16[1536,128]{1,0:T(8,128)(2,1)S(1)}) custom-call(s32[1,1,3,2,4]{4,3,2,1,0:T(2,128)S(1)} %bitcast.11, s32[1,1,3]{2,1,0:T(1,128)S(1)} %copy-done.4, f32[2,6,1024,128]{3,2,1,0:T(8,128)S(1)} %get-tuple-element.43.refs_2_, ...), custom_call_target="tpu_custom_call", output_to_operand_aliasing={{0}: (2, {}), {1}: (3, {})} | custom-call | flops 2147483648 | bytes 8388608 | tf_op jit(solution)/shard_map/far/pallas_call | solution.py:463
  32.6 4.2 %collective-permute-start.5 = (bf16[1536,128]{1,0:T(8,128)(2,1)S(1)}, bf16[1536,128]{1,0:T(8,128)(2,1)S(1)}, u32[]{:S(2)}, u32[]{:S(2)}) collective-permute-start(bf16[1536,128]{1,0:T(8,128)(2,1)S(1)} %get-tuple-element.51), channel_id=1, source_target_pairs={{8,16},{16,8},{24,32},{32,24},{40,48},{48,40},{56,64},{64,56},{72,... | collective-permute-start | bytes 1179656 | tf_op jit(solution)/shard_map/ppermute | solution.py:28
  36.8 2.7 %near.1 = (f32[2,6,1024,128]{3,2,1,0:T(8,128)S(1)}, f32[2,6,1024,128]{3,2,1,0:T(8,128)S(1)}, bf16[1536,128]{1,0:T(8,128)(2,1)S(1)}) custom-call(s32[1,1,3,2,4]{4,3,2,1,0:T(2,128)S(1)} %bitcast.12, s32[1,1,3]{2,1,0:T(1,128)S(1)} %copy-done.4, f32[2,6,1024,128]{3,2,1,0:T(8,128)S(1)} %get-tuple-element.46.refs_2_, ...), custom_call_target="tpu_custom_call", output_to_operand_aliasing={{0}: (2, {}), {1}: (3, {})} | custom-call | flops 2147483648 | bytes 8388608 | tf_op jit(solution)/shard_map/near/pallas_call | solution.py:463
  39.5 0.1 collective-permute-start.4
  39.6 4.2 %collective-permute-done.5.yb_ref.refs_3_ = bf16[1536,128]{1,0:T(8,128)(2,1)S(1)} collective-permute-done((bf16[1536,128]{1,0:T(8,128)(2,1)S(1)}, bf16[1536,128]{1,0:T(8,128)(2,1)S(1)}, u32[]{:S(2)}, u32[]{:S(2)}) %collective-permute-start.5) | collective-permute-done | bytes 393248 | tf_op jit(solution)/shard_map/ppermute | solution.py:28
  43.8 0.0 collective-permute-done.4.ya_ref.refs_2_
  43.8 0.2 strips.1
  44.0 0.1 collective-permute-start.6
  44.1 4.6 %collective-permute-start.7 = (bf16[1536,128]{1,0:T(8,128)(2,1)S(1)}, bf16[1536,128]{1,0:T(8,128)(2,1)S(1)}, u32[]{:S(2)}, u32[]{:S(2)}) collective-permute-start(bf16[1536,128]{1,0:T(8,128)(2,1)S(1)} %get-tuple-element.57), channel_id=1, source_target_pairs={{1,2},{2,1},{3,4},{4,3},{5,6},{6,5},{9,10},{10,9},{11,12},{12,11},... | collective-permute-start | bytes 1179656 | tf_op jit(solution)/shard_map/ppermute | solution.py:28
  48.6 4.1 %light.1.refs_4_ = f32[4,768,128]{2,1,0:T(8,128)S(1)} custom-call(bf16[48,128]{1,0:T(8,128)(2,1)S(1)} %get-tuple-element.52.meta_ref, bf16[1584,128]{1,0:T(8,128)(2,1)S(1)} %collective-permute-done.3.refs_4_.ya_ref, bf16[1584,128]{1,0:T(8,128)(2,1)S(1)} %collective-permute-done.2.refs_4_.yb_ref, f32[2,256,256]{2,1,0:T(8,128)S(1)} %copy-done.2), custom_call_target="tpu_custom_call" | custom-call | flops 8388608 | bytes 12582912 | tf_op jit(solution)/shard_map/light/pallas_call | solution.py:510
  52.7 1.8 %middle.1 = (f32[2,768,512]{2,1,0:T(8,128)}, f32[2,768,512]{2,1,0:T(8,128)}) custom-call(f32[2,768,512]{2,1,0:T(8,128)S(1)} %copy-done, f32[2,6,1024,128]{3,2,1,0:T(8,128)S(1)} %get-tuple-element.49.canvas_ref.refs_1_, bf16[1536,128]{1,0:T(8,128)(2,1)S(1)} %collective-permute-done.4.ya_ref.refs_2_, ...), custom_call_target="tpu_custom_call" | custom-call | flops 4194304 | bytes 10485760 | tf_op jit(solution)/shard_map/middle/pallas_call | solution.py:529
  54.5 2.8 %collective-permute-done.7.refs_6_ = bf16[1536,128]{1,0:T(8,128)(2,1)S(1)} collective-permute-done((bf16[1536,128]{1,0:T(8,128)(2,1)S(1)}, bf16[1536,128]{1,0:T(8,128)(2,1)S(1)}, u32[]{:S(2)}, u32[]{:S(2)}) %collective-permute-start.7) | collective-permute-done | bytes 393248 | tf_op jit(solution)/shard_map/ppermute | solution.py:28
  57.3 1.9 %rims.1 = (f32[2,768,512]{2,1,0:T(8,128)}, f32[2,768,512]{2,1,0:T(8,128)}) custom-call(f32[2,768,512]{2,1,0:T(8,128)S(1)} %copy-done, f32[2,6,1024,128]{3,2,1,0:T(8,128)S(1)} %get-tuple-element.49.canvas_ref.refs_1_, bf16[1536,128]{1,0:T(8,128)(2,1)S(1)} %collective-permute-done.4.ya_ref.refs_2_, ...), custom_call_target="tpu_custom_call", output_to_operand_aliasing={{0}: (7, {}), {1}: (8, {})} | custom-call | flops 4194304 | bytes 10485760 | tf_op jit(solution)/shard_map/rims/pallas_call | solution.py:529
  (13 shorter events, 0.0 us)
Async XLA Ops:
  0.6 13.6 %copy-start.4 = (s32[1,1,3]{2,1,0:T(1,128)S(1)}, s32[1,1,3]{2,1,0:T(1,128)}, u32[]{:S(2)}) copy-start(s32[1,1,3]{2,1,0:T(1,128)} %refs_1_.7) | copy-start | bytes 40
  0.6 12.4 %copy-start = (f32[2,768,512]{2,1,0:T(8,128)S(1)}, f32[2,768,512]{2,1,0:T(8,128)}, u32[]{:S(2)}) copy-start(f32[2,768,512]{2,1,0:T(8,128)} %refs_0_.3) | copy-start | bytes 9437188
  0.6 13.6 %copy-start.3 = (s32[1,1,3,4,2]{3,4,2,1,0:T(2,128)S(1)}, s32[1,1,3,4,2]{3,4,2,1,0:T(2,128)}, u32[]{:S(2)}) copy-start(s32[1,1,3,4,2]{3,4,2,1,0:T(2,128)} %param.8) | copy-start | bytes 292
  4.1 10.2 %copy-start.1 = (bf16[1,1,3,4,256,256]{5,4,3,2,1,0:T(8,128)(2,1)S(1)}, bf16[1,1,3,4,256,256]{5,4,3,2,1,0:T(8,128)(2,1)}, u32[]{:S(2)}) copy-start(bf16[1,1,3,4,256,256]{5,4,3,2,1,0:T(8,128)(2,1)} %param.7) | copy-start | bytes 4718596
  4.1 10.2 %copy-start.2 = (f32[2,256,256]{2,1,0:T(8,128)S(1)}, f32[2,256,256]{2,1,0:T(8,128)}, u32[]{:S(2)}) copy-start(f32[2,256,256]{2,1,0:T(8,128)} %probe_ref) | copy-start | bytes 1572868
  4.1 11.1 %collective-permute-start = (bf16[1552,128]{1,0:T(8,128)(2,1)}, bf16[1552,128]{1,0:T(8,128)(2,1)S(1)}, u32[]{:S(2)}, u32[]{:S(2)}) collective-permute-start(bf16[1552,128]{1,0:T(8,128)(2,1)} %get-tuple-element.37), channel_id=1, source_target_pairs={{0,1},{1,0},{2,3},{3,2},{4,5},{5,4},{6,7},{7,6},{8,9},{9,8},{10,11... | collective-permute-start | bytes 1191944 | tf_op jit(solution)/shard_map/ppermute | solution.py:28
  4.2 14.3 %collective-permute-start.1 = (bf16[1552,128]{1,0:T(8,128)(2,1)}, bf16[1552,128]{1,0:T(8,128)(2,1)S(1)}, u32[]{:S(2)}, u32[]{:S(2)}) collective-permute-start(bf16[1552,128]{1,0:T(8,128)(2,1)} %get-tuple-element.38), channel_id=1, source_target_pairs={{1,2},{2,1},{3,4},{4,3},{5,6},{6,5},{9,10},{10,9},{11,12},{12,11},... | collective-permute-start | bytes 1191944 | tf_op jit(solution)/shard_map/ppermute | solution.py:28
  14.3 4.2 %copy-start.5 = (bf16[16,128]{1,0:T(8,128)(2,1)S(1)}, bf16[16,128]{1,0:T(8,128)(2,1)}, u32[]{:S(2)}) copy-start(bf16[16,128]{1,0:T(8,128)(2,1)} %get-tuple-element.42.own_ref) | copy-start | bytes 12292
  18.7 11.3 %collective-permute-start.2 = (bf16[1584,128]{1,0:T(8,128)(2,1)S(1)}, bf16[1584,128]{1,0:T(8,128)(2,1)S(1)}, u32[]{:S(2)}, u32[]{:S(2)}) collective-permute-start(bf16[1584,128]{1,0:T(8,128)(2,1)S(1)} %get-tuple-element.45), channel_id=1, source_target_pairs={{8,16},{16,8},{24,32},{32,24},{40,48},{48,40},{56,64},{64,56},{72,... | collective-permute-start | bytes 1216520 | tf_op jit(solution)/shard_map/ppermute | solution.py:28
  22.9 13.9 %collective-permute-start.3 = (bf16[1584,128]{1,0:T(8,128)(2,1)S(1)}, bf16[1584,128]{1,0:T(8,128)(2,1)S(1)}, u32[]{:S(2)}, u32[]{:S(2)}) collective-permute-start(bf16[1584,128]{1,0:T(8,128)(2,1)S(1)} %get-tuple-element.48), channel_id=1, source_target_pairs={{0,8},{8,0},{16,24},{24,16},{32,40},{40,32},{48,56},{56,48},{64,72... | collective-permute-start | bytes 1216520 | tf_op jit(solution)/shard_map/ppermute | solution.py:28
  32.6 11.2 %collective-permute-start.5 = (bf16[1536,128]{1,0:T(8,128)(2,1)S(1)}, bf16[1536,128]{1,0:T(8,128)(2,1)S(1)}, u32[]{:S(2)}, u32[]{:S(2)}) collective-permute-start(bf16[1536,128]{1,0:T(8,128)(2,1)S(1)} %get-tuple-element.51), channel_id=1, source_target_pairs={{8,16},{16,8},{24,32},{32,24},{40,48},{48,40},{56,64},{64,56},{72,... | collective-permute-start | bytes 1179656 | tf_op jit(solution)/shard_map/ppermute | solution.py:28
  39.5 4.3 %collective-permute-start.4 = (bf16[1536,128]{1,0:T(8,128)(2,1)S(1)}, bf16[1536,128]{1,0:T(8,128)(2,1)S(1)}, u32[]{:S(2)}, u32[]{:S(2)}) collective-permute-start(bf16[1536,128]{1,0:T(8,128)(2,1)S(1)} %get-tuple-element.50), channel_id=1, source_target_pairs={{0,8},{8,0},{16,24},{24,16},{32,40},{40,32},{48,56},{56,48},{64,72... | collective-permute-start | bytes 1179656 | tf_op jit(solution)/shard_map/ppermute | solution.py:28
  44.0 10.6 %collective-permute-start.6 = (bf16[1536,128]{1,0:T(8,128)(2,1)S(1)}, bf16[1536,128]{1,0:T(8,128)(2,1)S(1)}, u32[]{:S(2)}, u32[]{:S(2)}) collective-permute-start(bf16[1536,128]{1,0:T(8,128)(2,1)S(1)} %get-tuple-element.56), channel_id=1, source_target_pairs={{0,1},{1,0},{2,3},{3,2},{4,5},{5,4},{6,7},{7,6},{8,9},{9,8},{10,11... | collective-permute-start | bytes 1179656 | tf_op jit(solution)/shard_map/ppermute | solution.py:28
  44.1 13.3 %collective-permute-start.7 = (bf16[1536,128]{1,0:T(8,128)(2,1)S(1)}, bf16[1536,128]{1,0:T(8,128)(2,1)S(1)}, u32[]{:S(2)}, u32[]{:S(2)}) collective-permute-start(bf16[1536,128]{1,0:T(8,128)(2,1)S(1)} %get-tuple-element.57), channel_id=1, source_target_pairs={{1,2},{2,1},{3,4},{4,3},{5,6},{6,5},{9,10},{10,9},{11,12},{12,11},... | collective-permute-start | bytes 1179656 | tf_op jit(solution)/shard_map/ppermute | solution.py:28
